TPU v7x, 256 devices: a whole 4x4x8 slice. The times are simulated.
256 devices in a mesh: nodes: 32 (over y, z), feat: 8 (over x, core).
Axes of the slice: x: 4, y: 4, z: 8, core: 2. Of those that a mesh axis runs over, the one named last changes fastest.
Arguments:
- features: bfloat16 [32768, 1024], P('nodes', 'feat'), may hold values from -6 to 6
- ghosts: int32 [1024, 2], P('nodes'), may hold values from 0 to 7, as said below
- slots: int32 [256, 24], P('nodes'), may hold values from 0 to 63
- tile_ids: int32 [256, 24], P('nodes'), may hold values from 0 to 15
- degrees: int32 [256], P('nodes'), may hold values from 1 to 24, 2048 in all
- tile_table: bfloat16 [16, 128, 128], replicated, may hold values from -0.5 to 0.5
- weight_one: bfloat16 [1024, 1024], P(None, 'feat'), may hold values from -0.1875 to 0.1875
- weight_two: bfloat16 [1024, 1024], P(None, 'feat'), may hold values from -0.1875 to 0.1875
- cotangent: bfloat16 [32768, 1024], P('nodes', 'feat'), may hold values from -0.15625 to 0.15625
Outputs:
- output: bfloat16 [32768, 1024], P('nodes', 'feat')
- grad_one: float32 [1024, 1024], P('nodes', 'feat')
- grad_two: float32 [1024, 1024], P('nodes', 'feat')
Inputs may be any that keep to these rules, and one draw needn't show every extreme that they name: `ghosts`: row d * 32 + p holds 2 distinct block indices of device p. The degrees sum to 2048; the largest is 24.
All inputs are finite; a program needn't handle non-finite values. No bound on the sum of `degrees` on one device may be relied on, other than what follows from the above.
Results may differ from a plain program's by a relative error of at most 0.0061.
Values may be sent and summed in bfloat16 or wider, within the bound.
A program may use at most 64 MiB of HBM per device.

v0:
```python
import jax
import jax.numpy as jnp
from jax import lax
from jax.sharding import PartitionSpec as P

entry_step = 8


def entry_weights(degrees, slot_width):
    position = lax.broadcasted_iota(jnp.int32, (degrees.shape[0], slot_width), 1)
    inverse_root = lax.rsqrt(degrees.astype(jnp.float32))[:, None]
    return jnp.where(position < degrees[:, None], inverse_root, 0.0)


def collect(ghost_rows, slots, tile_ids, weights, tile_table, passes):
    block_count = slots.shape[0]
    block_size = ghost_rows.shape[1]
    feat_width = ghost_rows.shape[2]

    def collect_advance(turn_index, running):
        first_entry = turn_index * entry_step
        near_ids = lax.dynamic_slice_in_dim(slots, first_entry, entry_step, 1)
        tile_pick = lax.dynamic_slice_in_dim(tile_ids, first_entry, entry_step, 1)
        entry_share = lax.dynamic_slice_in_dim(weights, first_entry, entry_step, 1)
        near_rows = ghost_rows[near_ids]
        picked = tile_table[tile_pick]
        products = jnp.einsum(
            "bkij,bkjf->bkif", picked, near_rows, preferred_element_type=jnp.float32
        )
        return running + jnp.sum(entry_share[:, :, None, None] * products, axis=1)

    start_value = jnp.zeros((block_count, block_size, feat_width), jnp.float32)
    return lax.fori_loop(0, passes, collect_advance, start_value)


def neighbours(values, requests, slots, tile_ids, weights, tile_table, passes):
    block_count = slots.shape[0]
    block_size = tile_table.shape[1]
    blocks = values.reshape(block_count, block_size, values.shape[1])
    outgoing = blocks[requests]
    arrived = lax.all_to_all(outgoing, "nodes", split_axis=0, concat_axis=0, tiled=True)
    flat_rows = arrived.reshape(-1, block_size, arrived.shape[3])
    running = collect(flat_rows, slots, tile_ids, weights, tile_table, passes)
    return (blocks.astype(jnp.float32) + running).astype(jnp.bfloat16).reshape(values.shape)


def scatter_back(grad_rows, requests, slots, tile_ids, weights, tile_table, passes, peer_count):
    block_count = slots.shape[0]
    block_size = tile_table.shape[1]
    feat_width = grad_rows.shape[1]
    blocks = grad_rows.reshape(block_count, block_size, feat_width)
    slot_total = requests.shape[0] * requests.shape[1]

    def scatter_advance(turn_index, running):
        first_entry = turn_index * entry_step
        near_ids = lax.dynamic_slice_in_dim(slots, first_entry, entry_step, 1)
        tile_pick = lax.dynamic_slice_in_dim(tile_ids, first_entry, entry_step, 1)
        entry_share = lax.dynamic_slice_in_dim(weights, first_entry, entry_step, 1)
        picked = tile_table[tile_pick]
        products = jnp.einsum("bkji,bjf->bkif", picked, blocks, preferred_element_type=jnp.float32)
        scaled = entry_share[:, :, None, None] * products
        return running + jax.ops.segment_sum(
            scaled.reshape(-1, block_size, feat_width),
            near_ids.reshape(-1),
            num_segments=slot_total,
        )

    start_value = jnp.zeros((slot_total, block_size, feat_width), jnp.float32)
    outbound = lax.fori_loop(0, passes, scatter_advance, start_value)
    outgoing = outbound.astype(jnp.bfloat16).reshape(peer_count, -1, block_size, feat_width)
    arrived = lax.all_to_all(outgoing, "nodes", split_axis=0, concat_axis=0, tiled=True)
    flat_rows = arrived.reshape(-1, block_size, arrived.shape[3]).astype(jnp.float32)
    running = jax.ops.segment_sum(flat_rows, requests.reshape(-1), num_segments=block_count)
    return (blocks.astype(jnp.float32) + running).reshape(grad_rows.shape)


def widen(values):
    return lax.all_gather(values, "feat", axis=1, tiled=True)


def weight_grad(wide_rows, local_rows):
    return lax.psum_scatter(
        lax.dot_general(
            wide_rows, local_rows, (((0,), (0,)), ((), ())), preferred_element_type=jnp.float32
        ),
        "nodes",
        scatter_dimension=0,
        tiled=True,
    )


def on_device(
    features, ghosts, slots, tile_ids, degrees, tile_table, weight_one, weight_two, cotangent
):
    peer_count = lax.axis_size("nodes")
    requests = lax.all_to_all(ghosts, "nodes", split_axis=0, concat_axis=0, tiled=True)
    weights = entry_weights(degrees, slots.shape[1])
    passes = slots.shape[1] // entry_step
    agg_one = neighbours(features, requests, slots, tile_ids, weights, tile_table, passes)
    wide_one = widen(agg_one)
    pre_one = jnp.dot(wide_one, weight_one, preferred_element_type=jnp.float32)
    hidden = jax.nn.silu(pre_one).astype(jnp.bfloat16)
    agg_two = neighbours(hidden, requests, slots, tile_ids, weights, tile_table, passes)
    wide_two = widen(agg_two)
    output = jnp.dot(wide_two, weight_two, preferred_element_type=jnp.float32).astype(jnp.bfloat16)
    grad_two = weight_grad(wide_two, cotangent)
    partial_terms = lax.dot_general(
        cotangent, weight_two, (((1,), (1,)), ((), ())), preferred_element_type=jnp.float32
    )
    grad_sum = lax.psum_scatter(partial_terms, "feat", scatter_dimension=1, tiled=True)
    grad_agg = grad_sum.astype(jnp.bfloat16)
    back_hidden = scatter_back(
        grad_agg, requests, slots, tile_ids, weights, tile_table, passes, peer_count
    )
    sigmoid_pre = jax.nn.sigmoid(pre_one)
    back_pre = (back_hidden * sigmoid_pre * (1.0 + pre_one * (1.0 - sigmoid_pre))).astype(
        jnp.bfloat16
    )
    grad_one = weight_grad(wide_one, back_pre)
    return (output, grad_one, grad_two)


def solution(mesh):
    return jax.shard_map(
        on_device,
        mesh=mesh,
        in_specs=(
            P("nodes", "feat"),
            P("nodes", None),
            P("nodes", None),
            P("nodes", None),
            P("nodes"),
            P(),
            P(None, "feat"),
            P(None, "feat"),
            P("nodes", "feat"),
        ),
        out_specs=(P("nodes", "feat"), P("nodes", "feat"), P("nodes", "feat")),
        check_vma=False,
    )
```

profile of v0, /device:TPU:1, one launch (start us, length us, event | category | flops | bytes accessed | tf_op | source)
XLA Modules:
  0.0 750.1 jit_solution(4377009243209254980)
XLA Ops:
  8.1 3.6 fusion.4
  12.5 20.5 %all_to_all.27 = s32[32,1,2]{2,1,0:T(1,128)S(1)} all-to-all(s32[32,1,2]{2,1,0:T(1,128)S(1)} %copy.19), channel_id=1, replica_groups=mesh['nodes'=32,'feat'=8] {'nodes'}, dimensions={0} | all-to-all | bytes 512 | tf_op jit(solution)/shard_map/all_to_all | solution.py:96
  33.3 2.1 gather_fusion.5
  35.4 4.9 all-to-all-start.1
  40.4 13.1 %reduce-scatter.4.cloned.1.call-done = f32[1024,128]{1,0:T(8,128)} async-done(((f32[1024,1024]{1,0:T(8,128)}), f32[1024,128]{1,0:T(8,128)}) %reduce-scatter.4.cloned.1.call-update) | async-done | bytes 524304 | tf_op jit(solution)/shard_map/reduce_scatter | solution.py:110
  54.6 2.5 broadcast.96
  57.1 53.7 %while.41 = (s32[]{:T(128)}, f32[64,128,128]{2,1,0:T(8,128)}, s32[8,24]{1,0:T(8,128)S(1)}, f32[8,24]{1,0:T(8,128)S(1)}, s32[8,24]{1,0:T(8,128)S(1)}, /*index=5*/...) while((s32[]{:T(128)}, f32[64,128,128]{2,1,0:T(8,128)}, ...), condition=%wide.region_9.10_spmd, body=%wide.region_7.9_spmd.sunk | while | flops 270533824 | bytes 23338668 | solution.py:69
  58.4 3.0 convolution_multiply_fusion.2
  61.3 13.7 %scatter_fusion = f32[64,128,128]{2,1,0:T(8,128)} fusion(f32[64,128,128]{2,1,0:T(8,128)} %get-tuple-element.629, s32[64]{0:T(128)S(1)} %reshape.230, f32[64,128,128]{2,1,0:T(8,128)} %bitcast.74), kind=kCustom, calls=%fused_computation.7.clone.1 | custom fusion | flops 1048576 | bytes 12583168 | tf_op jit(solution)/shard_map/while/body/eval_jaxpr/scatter-add | solution.py:62
  76.3 3.0 convolution_multiply_fusion.2
  79.3 13.6 %scatter_fusion = f32[64,128,128]{2,1,0:T(8,128)} fusion(f32[64,128,128]{2,1,0:T(8,128)} %get-tuple-element.629, s32[64]{0:T(128)S(1)} %reshape.230, f32[64,128,128]{2,1,0:T(8,128)} %bitcast.74), kind=kCustom, calls=%fused_computation.7.clone.1 | custom fusion | flops 1048576 | bytes 12583168 | tf_op jit(solution)/shard_map/while/body/eval_jaxpr/scatter-add | solution.py:62
  94.2 3.0 convolution_multiply_fusion.2
  97.1 13.7 %scatter_fusion = f32[64,128,128]{2,1,0:T(8,128)} fusion(f32[64,128,128]{2,1,0:T(8,128)} %get-tuple-element.629, s32[64]{0:T(128)S(1)} %reshape.230, f32[64,128,128]{2,1,0:T(8,128)} %bitcast.74), kind=kCustom, calls=%fused_computation.7.clone.1 | custom fusion | flops 1048576 | bytes 12583168 | tf_op jit(solution)/shard_map/while/body/eval_jaxpr/scatter-add | solution.py:62
  110.8 3.9 convert_element_type.48
  114.7 9.5 %all-to-all-start.3 = ((bf16[32,2,128,128]{3,2,1,0:T(8,128)(2,1)}), bf16[32,2,128,128]{3,2,1,0:T(8,128)(2,1)}, u32[]{:S(2)}, u32[]{:S(2)}) async-start(bf16[32,2,128,128]{3,2,1,0:T(8,128)(2,1)} %bitcast.15), calls=%async_computation.4 | async-start | bytes 4194304 | tf_op jit(solution)/shard_map/all_to_all | solution.py:71
  124.2 30.6 %while.42 = (s32[]{:T(128)}, f32[8,128,128]{2,1,0:T(8,128)}, f32[8,24]{1,0:T(8,128)S(1)}, s32[8,24]{1,0:T(8,128)S(1)}, bf16[16,128,128]{2,1,0:T(8,128)(2,1)S(1)}...) while((s32[]{:T(128)}, f32[8,128,128]{2,1,0:T(8,128)}, ...), condition=%wide.region_2.3_spmd.clone, body=%wide.region_0.2_spmd.clone.sunk | while | flops 270666112 | bytes 14692277 | solution.py:33
  125.5 3.7 gather_fusion.2
  129.3 3.1 multiply_reduce_fusion.4
  135.5 3.7 gather_fusion.2
  139.3 3.1 multiply_reduce_fusion.4
  142.5 2.1 select_add_fusion.4
  145.8 3.7 gather_fusion.2
  149.6 3.1 multiply_reduce_fusion.4
  152.7 2.1 select_add_fusion.4
  158.0 12.1 %all-to-all-done.3 = bf16[32,2,128,128]{3,2,1,0:T(8,128)(2,1)} async-done(((bf16[32,2,128,128]{3,2,1,0:T(8,128)(2,1)}), bf16[32,2,128,128]{3,2,1,0:T(8,128)(2,1)}, u32[]{:S(2)}, u32[]{:S(2)}) %all-to-all-start.3) | async-done | bytes 2097184 | tf_op jit(solution)/shard_map/all_to_all | solution.py:71
  170.1 4.2 bitcast_convert_fusion
  174.2 8.8 %scatter_fusion.1 = f32[8,128,128]{2,1,0:T(8,128)S(1)} fusion(f32[8,128,128]{2,1,0:T(8,128)S(1)} %convert_element_type.47, s32[64]{0:T(128)S(1)} %reshape.162, f32[64,128,128]{2,1,0:T(8,128)} %bitcast_convert_fusion), kind=kCustom, calls=%fused_computation.8 | custom fusion | flops 1048576 | bytes 12583168 | tf_op jit(solution)/shard_map/scatter-add | solution.py:73
  183.0 5.9 all-gather.3.cloned.1.call-done
  189.0 3.0 fusion.2
  192.0 2.2 gather_fusion.6
  194.1 9.6 %all-to-all-start.2 = ((bf16[32,2,128,128]{3,2,1,0:T(8,128)(2,1)}), bf16[32,2,128,128]{3,2,1,0:T(8,128)(2,1)S(1)}, u32[]{:S(2)}, u32[]{:S(2)}) async-start(bf16[32,2,128,128]{3,2,1,0:T(8,128)(2,1)} %bitcast.86), calls=%async_computation.2 | async-start | bytes 4194304 | tf_op jit(solution)/shard_map/all_to_all | solution.py:41
  203.9 48.7 %all-to-all-done.2 = bf16[32,2,128,128]{3,2,1,0:T(8,128)(2,1)S(1)} async-done(((bf16[32,2,128,128]{3,2,1,0:T(8,128)(2,1)}), bf16[32,2,128,128]{3,2,1,0:T(8,128)(2,1)S(1)}, u32[]{:S(2)}, u32[]{:S(2)}) %all-to-all-start.2) | async-done | bytes 2097184 | tf_op jit(solution)/shard_map/all_to_all | solution.py:41
  252.6 31.2 %while.43 = (s32[]{:T(128)}, f32[8,128,128]{2,1,0:T(8,128)}, f32[8,24]{1,0:T(8,128)S(1)}, s32[8,24]{1,0:T(8,128)S(1)}, bf16[16,128,128]{2,1,0:T(8,128)(2,1)S(1)}...) while((s32[]{:T(128)}, f32[8,128,128]{2,1,0:T(8,128)}, ...), condition=%wide.region_5.6_spmd.clone, body=%wide.region_3.5_spmd.clone.sunk | while | flops 270666112 | bytes 14692277 | solution.py:33
  252.8 2.2 gather_fusion.3
  255.0 2.1 gather_fusion.4
  257.2 3.8 multiply_reduce_fusion.5
  263.1 2.2 gather_fusion.3
  265.3 2.1 gather_fusion.4
  267.5 3.8 multiply_reduce_fusion.5
  271.3 2.1 select_add_fusion.5
  273.5 2.2 gather_fusion.3
  275.8 2.1 gather_fusion.4
  278.0 3.8 multiply_reduce_fusion.5
  285.7 3.1 fusion.5
  288.9 26.0 %all-gather.5.cloned.1.call-done = bf16[1024,1024]{1,0:T(8,128)(2,1)} async-done(((bf16[1024,128]{1,0:T(8,128)(2,1)}), bf16[1024,1024]{1,0:T(8,128)(2,1)}) %all-gather.5.cloned.1.call-update) | async-done | bytes 2097168 | tf_op jit(solution)/shard_map/all_gather | solution.py:78
  314.9 3.3 fusion.6
  319.7 207.9 %reduce-scatter.6.cloned.1.call-done = f32[32,128]{1,0:T(8,128)} async-done(((f32[1024,128]{1,0:T(8,128)}), f32[32,128]{1,0:T(8,128)}) %reduce-scatter.6.cloned.1.call-update) | async-done | bytes 16400 | tf_op jit(solution)/shard_map/reduce_scatter | solution.py:82
  527.5 216.1 %reduce-scatter.8.cloned.1.call-done = f32[32,128]{1,0:T(8,128)} async-done(((f32[1024,128]{1,0:T(8,128)}), f32[32,128]{1,0:T(8,128)}) %reduce-scatter.8.cloned.1.call-update) | async-done | bytes 16400 | tf_op jit(solution)/shard_map/reduce_scatter | solution.py:82
  (109 shorter events, 24.4 us)
Async XLA Ops:
  7.2 1.0 copy-start
  7.2 46.3 %reduce-scatter.4.cloned.1.call-start = ((), (), s32[]{:S(2)}) async-start(), calls=%async_computation.9 | async-start | bytes 4718592 | tf_op jit(solution)/shard_map/reduce_scatter | solution.py:110
  11.7 0.7 copy-start.7
  11.7 21.5 %copy-start.2 = (bf16[1024,128]{1,0:T(8,128)(2,1)S(1)}, bf16[1024,128]{1,0:T(8,128)(2,1)}, u32[]{:S(2)}) copy-start(bf16[1024,128]{1,0:T(8,128)(2,1)} %param.15) | copy-start | bytes 786436
  35.4 4.9 copy-start.8
  35.4 79.3 %all-to-all-start.1 = ((bf16[32,2,128,128]{3,2,1,0:T(8,128)(2,1)}), bf16[32,2,128,128]{3,2,1,0:T(8,128)(2,1)}, u32[]{:S(2)}, u32[]{:S(2)}) async-start(bf16[32,2,128,128]{3,2,1,0:T(8,128)(2,1)} %bitcast.7), calls=%async_computation.1 | async-start | bytes 4194304 | tf_op jit(solution)/shard_map/all_to_all | solution.py:41
  54.5 2.5 copy-start.1
  54.6 2.5 copy-start.5
  54.6 2.5 copy-start.6
  114.7 55.4 %all-to-all-start.3 = ((bf16[32,2,128,128]{3,2,1,0:T(8,128)(2,1)}), bf16[32,2,128,128]{3,2,1,0:T(8,128)(2,1)}, u32[]{:S(2)}, u32[]{:S(2)}) async-start(bf16[32,2,128,128]{3,2,1,0:T(8,128)(2,1)} %bitcast.15), calls=%async_computation.4 | async-start | bytes 4194304 | tf_op jit(solution)/shard_map/all_to_all | solution.py:71
  124.2 64.8 %all-gather.3.cloned.1.call-start = ((), (), s32[]{:S(2)}) async-start(), calls=%async_computation.7 | async-start | bytes 2359296 | tf_op jit(solution)/shard_map/all_gather | solution.py:78
  174.2 14.7 %copy-start.9 = (bf16[1024,128]{1,0:T(8,128)(2,1)S(1)}, bf16[1024,128]{1,0:T(8,128)(2,1)}, u32[]{:S(2)}) copy-start(bf16[1024,128]{1,0:T(8,128)(2,1)} %param.21) | copy-start | bytes 786436
  194.1 58.5 %all-to-all-start.2 = ((bf16[32,2,128,128]{3,2,1,0:T(8,128)(2,1)}), bf16[32,2,128,128]{3,2,1,0:T(8,128)(2,1)S(1)}, u32[]{:S(2)}, u32[]{:S(2)}) async-start(bf16[32,2,128,128]{3,2,1,0:T(8,128)(2,1)} %bitcast.86), calls=%async_computation.2 | async-start | bytes 4194304 | tf_op jit(solution)/shard_map/all_to_all | solution.py:41
  203.7 111.2 %all-gather.5.cloned.1.call-start = ((), (), s32[]{:S(2)}) async-start(), calls=%async_computation.8 | async-start | bytes 2359296 | tf_op jit(solution)/shard_map/all_gather | solution.py:78
  285.6 241.9 %reduce-scatter.6.cloned.1.call-start = ((), (), s32[]{:S(2)}) async-start(), calls=%async_computation.10 | async-start | bytes 540672 | tf_op jit(solution)/shard_map/reduce_scatter | solution.py:82
  288.8 29.4 %copy-start.4 = (bf16[1024,128]{1,0:T(8,128)(2,1)S(1)}, bf16[1024,128]{1,0:T(8,128)(2,1)}, u32[]{:S(2)}) copy-start(bf16[1024,128]{1,0:T(8,128)(2,1)} %param.22) | copy-start | bytes 786436
  288.8 454.7 %reduce-scatter.8.cloned.1.call-start = ((), (), s32[]{:S(2)}) async-start(), calls=%async_computation.11 | async-start | bytes 540672 | tf_op jit(solution)/shard_map/reduce_scatter | solution.py:82
  314.9 3.3 copy-start.3
Sparse Core Ops, SparseCore 0:
  11.9 41.5 reduce-scatter.3
  156.7 32.1 all-gather.2
  285.7 29.1 all-gather.4
  319.1 208.3 reduce-scatter.5
  532.2 211.3 reduce-scatter.7
where the time goes:
time: 756 us; the launch traced here: 750 us
  waiting for transfers between devices  530 us (70%)
  other arithmetic  76.2 us (10%)
  matrix products  44.1 us (6%)
  local copies, waits for them, and re-layouts  41.3 us (5%)
  starting transfers between devices  24.3 us (3%)
  blocking collectives  20.5 us (3%)
  between operations  14 us (2%)
    reduce_scatter x2, waiting for transfers between devices, weight_grad(): lax.psum_scatter(lax.dot_general(wide_rows, local_rows, (((0,), (0,)), ((...  424 us
    all_to_all x2, waiting for transfers between devices, neighbours(): lax.all_to_all(outgoing, 'nodes', split_axis=0, concat_axis=0, tiled=True)  48.7 us
    scatter-add x3, other arithmetic, scatter_advance(): jax.ops.segment_sum(scaled.reshape(-1, block_size, feat_width), near_ids....  41 us
    all_gather x2, waiting for transfers between devices, widen(): return lax.all_gather(values, 'feat', axis=1, tiled=True)  31.9 us
    dot_general x6, matrix products, collect_advance(): jnp.einsum('bkij,bkjf->bkif', picked, near_rows, preferred_element_type=j...  20.7 us
    all_to_all x1, blocking collectives, on_device(): lax.all_to_all(ghosts, 'nodes', split_axis=0, concat_axis=0, tiled=True)  20.5 us
    gather x6, local copies, waits for them, and re-layouts, collect_advance(): near_rows = ghost_rows[near_ids]  17.6 us
  transfers between devices with their start and end apart: 8, of which 7 were waited for; matrix products, arithmetic and copies ran while one was open for 16% of the time, Pallas kernels for 0%

commit v1 on v0

--- a/solution.py
+++ b/solution.py
@@ -79,14 +79,13 @@
 
 
 def weight_grad(wide_rows, local_rows):
-    return lax.psum_scatter(
-        lax.dot_general(
-            wide_rows, local_rows, (((0,), (0,)), ((), ())), preferred_element_type=jnp.float32
-        ),
-        "nodes",
-        scatter_dimension=0,
-        tiled=True,
+    shares = lax.dot_general(
+        wide_rows, local_rows, (((0,), (0,)), ((), ())), preferred_element_type=jnp.float32
     )
+    peer_count = lax.axis_size("nodes")
+    shares = shares.reshape(peer_count, -1, shares.shape[1])
+    arrived = lax.all_to_all(shares, "nodes", split_axis=0, concat_axis=0, tiled=True)
+    return jnp.sum(arrived, axis=0)
 
 
 def on_device(

time: 756 us -> 354 us (0.47)
  waiting for transfers between devices: 530 us -> 109 us
  starting transfers between devices: 24.3 us -> 41.6 us
    reduce_scatter x2 -> x0, waiting for transfers between devices: 424 us -> none  [weight_grad(): lax.psum_scatter(lax.dot_general(wide_rows, local_rows, (((0,), (0,)), ((...]
    all_to_all x0 -> x2, starting transfers between devices: none -> 17.1 us  [weight_grad(): lax.all_to_all(shares, 'nodes', split_axis=0, concat_axis=0, tiled=True)]
    all_to_all x0 -> x2, waiting for transfers between devices: none -> 11 us  [weight_grad(): lax.all_to_all(shares, 'nodes', split_axis=0, concat_axis=0, tiled=True)]
  transfers between devices with their start and end apart: 8 -> 8, of which waited for: 7 -> 6; matrix products, arithmetic and copies ran while one was open for 16% -> 34% of each run, Pallas kernels for 0% -> 0%
where the time goes in v1:
time: 354 us; the launch traced here: 349 us
  waiting for transfers between devices  109 us (31%)
  other arithmetic  77.1 us (22%)
  matrix products  45.1 us (13%)
  starting transfers between devices  41.6 us (12%)
  local copies, waits for them, and re-layouts  41.2 us (12%)
  blocking collectives  20.5 us (6%)
  between operations  13.9 us (4%)
    all_to_all x2, waiting for transfers between devices, neighbours(): lax.all_to_all(outgoing, 'nodes', split_axis=0, concat_axis=0, tiled=True)  48.7 us
    scatter-add x3, other arithmetic, scatter_advance(): jax.ops.segment_sum(scaled.reshape(-1, block_size, feat_width), near_ids....  40.7 us
    all_gather x2, waiting for transfers between devices, widen(): return lax.all_gather(values, 'feat', axis=1, tiled=True)  24.5 us
    dot_general x6, matrix products, collect_advance(): jnp.einsum('bkij,bkjf->bkif', picked, near_rows, preferred_element_type=j...  20.8 us
    all_to_all x1, blocking collectives, on_device(): lax.all_to_all(ghosts, 'nodes', split_axis=0, concat_axis=0, tiled=True)  20.5 us
    gather x6, local copies, waits for them, and re-layouts, collect_advance(): near_rows = ghost_rows[near_ids]  17.6 us
    all_to_all x2, starting transfers between devices, weight_grad(): lax.all_to_all(shares, 'nodes', split_axis=0, concat_axis=0, tiled=True)  17.1 us
    all_to_all x2, starting transfers between devices, neighbours(): lax.all_to_all(outgoing, 'nodes', split_axis=0, concat_axis=0, tiled=True)  14.5 us
  transfers between devices with their start and end apart: 8, of which 6 were waited for; matrix products, arithmetic and copies ran while one was open for 34% of the time, Pallas kernels for 0%

profile of v1, /device:TPU:1, one launch (start us, length us, event | category | flops | bytes accessed | tf_op | source)
XLA Modules:
  0.0 348.9 jit_solution(16912315060916707319)
XLA Ops:
  8.1 3.6 %fusion.4 = f32[1024,1024]{1,0:T(8,128)} fusion(bf16[1024,128]{1,0:T(8,128)(2,1)S(1)} %copy-done, bf16[1024,128]{1,0:T(8,128)(2,1)} %param.22), kind=kOutput, calls=%fused_computation.43 | convolution fusion | flops 268435456 | bytes 4718592 | tf_op jit(solution)/shard_map/dot_general | solution.py:106
  12.5 20.5 %all_to_all.37 = s32[32,1,2]{2,1,0:T(1,128)S(1)} all-to-all(s32[32,1,2]{2,1,0:T(1,128)S(1)} %copy.19), channel_id=1, replica_groups=mesh['nodes'=32,'feat'=8] {'nodes'}, dimensions={0} | all-to-all | bytes 512 | tf_op jit(solution)/shard_map/all_to_all | solution.py:95
  33.3 2.1 gather_fusion.5
  35.4 4.9 %all-to-all-start.1 = ((bf16[32,2,128,128]{3,2,1,0:T(8,128)(2,1)}), bf16[32,2,128,128]{3,2,1,0:T(8,128)(2,1)}, u32[]{:S(2)}, u32[]{:S(2)}) async-start(bf16[32,2,128,128]{3,2,1,0:T(8,128)(2,1)} %bitcast.7), calls=%async_computation.1 | async-start | bytes 4194304 | tf_op jit(solution)/shard_map/all_to_all | solution.py:41
  40.4 13.1 %reduce-scatter.2.cloned.1.call-done = f32[1024,128]{1,0:T(8,128)} async-done(((f32[1024,1024]{1,0:T(8,128)}), f32[1024,128]{1,0:T(8,128)}) %reduce-scatter.2.cloned.1.call-update) | async-done | bytes 524304 | tf_op jit(solution)/shard_map/reduce_scatter | solution.py:109
  54.6 2.5 broadcast.96
  57.1 53.4 %while.41 = (s32[]{:T(128)}, f32[64,128,128]{2,1,0:T(8,128)}, s32[8,24]{1,0:T(8,128)S(1)}, f32[8,24]{1,0:T(8,128)S(1)}, s32[8,24]{1,0:T(8,128)S(1)}, /*index=5*/...) while((s32[]{:T(128)}, f32[64,128,128]{2,1,0:T(8,128)}, ...), condition=%wide.region_9.10_spmd, body=%wide.region_7.9_spmd.sunk | while | flops 270533824 | bytes 23338668 | solution.py:69
  58.4 3.0 convolution_multiply_fusion.2
  61.3 13.6 %scatter_fusion = f32[64,128,128]{2,1,0:T(8,128)} fusion(f32[64,128,128]{2,1,0:T(8,128)} %get-tuple-element.629, s32[64]{0:T(128)S(1)} %reshape.238, f32[64,128,128]{2,1,0:T(8,128)} %bitcast.76), kind=kCustom, calls=%fused_computation.7.clone.1 | custom fusion | flops 1048576 | bytes 12583168 | tf_op jit(solution)/shard_map/while/body/eval_jaxpr/scatter-add | solution.py:62
  76.2 3.0 convolution_multiply_fusion.2
  79.2 13.5 %scatter_fusion = f32[64,128,128]{2,1,0:T(8,128)} fusion(f32[64,128,128]{2,1,0:T(8,128)} %get-tuple-element.629, s32[64]{0:T(128)S(1)} %reshape.238, f32[64,128,128]{2,1,0:T(8,128)} %bitcast.76), kind=kCustom, calls=%fused_computation.7.clone.1 | custom fusion | flops 1048576 | bytes 12583168 | tf_op jit(solution)/shard_map/while/body/eval_jaxpr/scatter-add | solution.py:62
  93.9 3.0 convolution_multiply_fusion.2
  96.9 13.6 %scatter_fusion = f32[64,128,128]{2,1,0:T(8,128)} fusion(f32[64,128,128]{2,1,0:T(8,128)} %get-tuple-element.629, s32[64]{0:T(128)S(1)} %reshape.238, f32[64,128,128]{2,1,0:T(8,128)} %bitcast.76), kind=kCustom, calls=%fused_computation.7.clone.1 | custom fusion | flops 1048576 | bytes 12583168 | tf_op jit(solution)/shard_map/while/body/eval_jaxpr/scatter-add | solution.py:62
  110.5 3.9 %convert_element_type.48 = bf16[64,128,128]{2,1,0:T(8,128)(2,1)} convert(f32[64,128,128]{2,1,0:T(8,128)} %get-tuple-element.377) | non-fusion elementwise | flops 1048576 | bytes 6291456 | tf_op jit(solution)/shard_map/convert_element_type | solution.py:70
  114.4 9.7 %all-to-all-start.3 = ((bf16[32,2,128,128]{3,2,1,0:T(8,128)(2,1)}), bf16[32,2,128,128]{3,2,1,0:T(8,128)(2,1)}, u32[]{:S(2)}, u32[]{:S(2)}) async-start(bf16[32,2,128,128]{3,2,1,0:T(8,128)(2,1)} %bitcast.15), calls=%async_computation.4 | async-start | bytes 4194304 | tf_op jit(solution)/shard_map/all_to_all | solution.py:71
  124.2 30.5 %while.42 = (s32[]{:T(128)}, f32[8,128,128]{2,1,0:T(8,128)}, f32[8,24]{1,0:T(8,128)S(1)}, s32[8,24]{1,0:T(8,128)S(1)}, bf16[16,128,128]{2,1,0:T(8,128)(2,1)S(1)}...) while((s32[]{:T(128)}, f32[8,128,128]{2,1,0:T(8,128)}, ...), condition=%wide.region_2.3_spmd.clone, body=%wide.region_0.2_spmd.clone.sunk | while | flops 270666112 | bytes 14692277 | solution.py:33
  125.4 3.7 %gather_fusion.2 = bf16[64,128,128]{2,1,0:T(8,128)(2,1)} fusion(bf16[64,128,128]{2,1,0:T(8,128)(2,1)} %get-tuple-element.678, s32[1024]{0:T(1024)S(1)} %pad_clamp_fusion.13), kind=kCustom, calls=%fused_computation.1.clone.clone.1 | custom fusion | bytes 4194560 | tf_op jit(solution)/shard_map/while/body/eval_jaxpr/gather | solution.py:25
  129.2 3.1 multiply_reduce_fusion.4
  135.5 3.7 %gather_fusion.2 = bf16[64,128,128]{2,1,0:T(8,128)(2,1)} fusion(bf16[64,128,128]{2,1,0:T(8,128)(2,1)} %get-tuple-element.678, s32[1024]{0:T(1024)S(1)} %pad_clamp_fusion.13), kind=kCustom, calls=%fused_computation.1.clone.clone.1 | custom fusion | bytes 4194560 | tf_op jit(solution)/shard_map/while/body/eval_jaxpr/gather | solution.py:25
  139.3 3.1 multiply_reduce_fusion.4
  142.4 2.1 select_add_fusion.4
  145.7 3.7 %gather_fusion.2 = bf16[64,128,128]{2,1,0:T(8,128)(2,1)} fusion(bf16[64,128,128]{2,1,0:T(8,128)(2,1)} %get-tuple-element.678, s32[1024]{0:T(1024)S(1)} %pad_clamp_fusion.13), kind=kCustom, calls=%fused_computation.1.clone.clone.1 | custom fusion | bytes 4194560 | tf_op jit(solution)/shard_map/while/body/eval_jaxpr/gather | solution.py:25
  149.5 3.1 multiply_reduce_fusion.4
  157.9 12.1 %all-to-all-done.3 = bf16[32,2,128,128]{3,2,1,0:T(8,128)(2,1)} async-done(((bf16[32,2,128,128]{3,2,1,0:T(8,128)(2,1)}), bf16[32,2,128,128]{3,2,1,0:T(8,128)(2,1)}, u32[]{:S(2)}, u32[]{:S(2)}) %all-to-all-start.3) | async-done | bytes 2097184 | tf_op jit(solution)/shard_map/all_to_all | solution.py:71
  170.0 4.2 %bitcast_convert_fusion = f32[64,128,128]{2,1,0:T(8,128)} fusion(bf16[32,2,128,128]{3,2,1,0:T(8,128)(2,1)} %all-to-all-done.3), kind=kLoop, calls=%fused_computation.29 | loop fusion | flops 1048576 | bytes 6291456 | tf_op jit(solution)/shard_map/convert_element_type | solution.py:72
  174.2 8.8 %scatter_fusion.1 = f32[8,128,128]{2,1,0:T(8,128)S(1)} fusion(f32[8,128,128]{2,1,0:T(8,128)S(1)} %convert_element_type.47, s32[64]{0:T(128)S(1)} %reshape.170, f32[64,128,128]{2,1,0:T(8,128)} %bitcast_convert_fusion), kind=kCustom, calls=%fused_computation.8 | custom fusion | flops 1048576 | bytes 12583168 | tf_op jit(solution)/shard_map/scatter-add | solution.py:73
  183.0 5.9 %all-gather.3.cloned.1.call-done = bf16[1024,1024]{1,0:T(8,128)(2,1)} async-done(((bf16[1024,128]{1,0:T(8,128)(2,1)}), bf16[1024,1024]{1,0:T(8,128)(2,1)}) %all-gather.3.cloned.1.call-update) | async-done | bytes 2097168 | tf_op jit(solution)/shard_map/all_gather | solution.py:78
  188.9 3.0 fusion.2
  191.9 2.1 gather_fusion.6
  194.0 9.6 %all-to-all-start.2 = ((bf16[32,2,128,128]{3,2,1,0:T(8,128)(2,1)}), bf16[32,2,128,128]{3,2,1,0:T(8,128)(2,1)S(1)}, u32[]{:S(2)}, u32[]{:S(2)}) async-start(bf16[32,2,128,128]{3,2,1,0:T(8,128)(2,1)} %bitcast.88), calls=%async_computation.2 | async-start | bytes 4194304 | tf_op jit(solution)/shard_map/all_to_all | solution.py:41
  203.9 48.7 %all-to-all-done.2 = bf16[32,2,128,128]{3,2,1,0:T(8,128)(2,1)S(1)} async-done(((bf16[32,2,128,128]{3,2,1,0:T(8,128)(2,1)}), bf16[32,2,128,128]{3,2,1,0:T(8,128)(2,1)S(1)}, u32[]{:S(2)}, u32[]{:S(2)}) %all-to-all-start.2) | async-done | bytes 2097184 | tf_op jit(solution)/shard_map/all_to_all | solution.py:41
  252.5 31.2 %while.43 = (s32[]{:T(128)}, f32[8,128,128]{2,1,0:T(8,128)}, f32[8,24]{1,0:T(8,128)S(1)}, s32[8,24]{1,0:T(8,128)S(1)}, bf16[16,128,128]{2,1,0:T(8,128)(2,1)S(1)}...) while((s32[]{:T(128)}, f32[8,128,128]{2,1,0:T(8,128)}, ...), condition=%wide.region_5.6_spmd.clone, body=%wide.region_3.5_spmd.clone.sunk | while | flops 270666112 | bytes 14692277 | solution.py:33
  252.7 2.1 gather_fusion.3
  254.9 2.1 gather_fusion.4
  257.2 3.8 %multiply_reduce_fusion.5 = f32[8,128,128]{2,1,0:T(8,128)} fusion(bf16[8,8,128,128]{3,2,1,0:T(8,128)(2,1)} %bitcast.80, bf16[8,8,128,128]{3,2,1,0:T(8,128)(2,1)} %bitcast.82, f32[8,8]{1,0:T(8,128)S(1)} %constant_dynamic-slice_fusion.9), kind=kOutput, calls=%fused_computation.22.clone.1 | convolution fusion | flops 270401536 | bytes 4718848 | tf_op jit(solution)/shard_map/while/body/eval_jaxpr/bkij,bkjf->bkif/dot_general | solution.py:27
  263.0 2.1 gather_fusion.3
  265.2 2.1 gather_fusion.4
  267.4 3.8 %multiply_reduce_fusion.5 = f32[8,128,128]{2,1,0:T(8,128)} fusion(bf16[8,8,128,128]{3,2,1,0:T(8,128)(2,1)} %bitcast.80, bf16[8,8,128,128]{3,2,1,0:T(8,128)(2,1)} %bitcast.82, f32[8,8]{1,0:T(8,128)S(1)} %constant_dynamic-slice_fusion.9), kind=kOutput, calls=%fused_computation.22.clone.1 | convolution fusion | flops 270401536 | bytes 4718848 | tf_op jit(solution)/shard_map/while/body/eval_jaxpr/bkij,bkjf->bkif/dot_general | solution.py:27
  273.5 2.1 gather_fusion.3
  275.7 2.1 gather_fusion.4
  277.9 3.8 %multiply_reduce_fusion.5 = f32[8,128,128]{2,1,0:T(8,128)} fusion(bf16[8,8,128,128]{3,2,1,0:T(8,128)(2,1)} %bitcast.80, bf16[8,8,128,128]{3,2,1,0:T(8,128)(2,1)} %bitcast.82, f32[8,8]{1,0:T(8,128)S(1)} %constant_dynamic-slice_fusion.9), kind=kOutput, calls=%fused_computation.22.clone.1 | convolution fusion | flops 270401536 | bytes 4718848 | tf_op jit(solution)/shard_map/while/body/eval_jaxpr/bkij,bkjf->bkif/dot_general | solution.py:27
  285.6 3.1 fusion.5
  288.7 7.5 %all-to-all-start.4 = ((f32[32,32,128]{2,1,0:T(8,128)}), f32[32,32,128]{2,1,0:T(8,128)S(1)}, u32[]{:S(2)}, u32[]{:S(2)}) async-start(f32[32,32,128]{2,1,0:T(8,128)} %bitcast.18), calls=%async_computation.5 | async-start | bytes 1048576 | tf_op jit(solution)/shard_map/all_to_all | solution.py:87
  296.2 18.6 %all-gather.5.cloned.1.call-done = bf16[1024,1024]{1,0:T(8,128)(2,1)} async-done(((bf16[1024,128]{1,0:T(8,128)(2,1)}), bf16[1024,1024]{1,0:T(8,128)(2,1)}) %all-gather.5.cloned.1.call-update) | async-done | bytes 2097168 | tf_op jit(solution)/shard_map/all_gather | solution.py:78
  314.9 3.3 fusion.6
  318.1 9.6 %all-to-all-start.5 = ((f32[32,32,128]{2,1,0:T(8,128)}), f32[32,32,128]{2,1,0:T(8,128)S(1)}, u32[]{:S(2)}, u32[]{:S(2)}) async-start(f32[32,32,128]{2,1,0:T(8,128)} %bitcast.19), calls=%async_computation.6 | async-start | bytes 1048576 | tf_op jit(solution)/shard_map/all_to_all | solution.py:87
  328.4 2.4 convolution_convert_fusion
  330.7 11.0 %all-to-all-done.5 = f32[32,32,128]{2,1,0:T(8,128)S(1)} async-done(((f32[32,32,128]{2,1,0:T(8,128)}), f32[32,32,128]{2,1,0:T(8,128)S(1)}, u32[]{:S(2)}, u32[]{:S(2)}) %all-to-all-start.5) | async-done | bytes 524320 | tf_op jit(solution)/shard_map/all_to_all | solution.py:87
  (107 shorter events, 28.3 us)
Async XLA Ops:
  7.2 1.0 copy-start
  7.2 46.3 %reduce-scatter.2.cloned.1.call-start = ((), (), s32[]{:S(2)}) async-start(), calls=%async_computation.9 | async-start | bytes 4718592 | tf_op jit(solution)/shard_map/reduce_scatter | solution.py:109
  11.7 0.7 copy-start.6
  11.7 21.5 %copy-start.2 = (bf16[1024,128]{1,0:T(8,128)(2,1)S(1)}, bf16[1024,128]{1,0:T(8,128)(2,1)}, u32[]{:S(2)}) copy-start(bf16[1024,128]{1,0:T(8,128)(2,1)} %param.15) | copy-start | bytes 786436
  35.4 4.9 %copy-start.7 = (s32[8]{0:T(128)S(1)}, s32[8]{0:T(128)}, u32[]{:S(2)}) copy-start(s32[8]{0:T(128)} %param.19) | copy-start | bytes 100
  35.4 79.0 %all-to-all-start.1 = ((bf16[32,2,128,128]{3,2,1,0:T(8,128)(2,1)}), bf16[32,2,128,128]{3,2,1,0:T(8,128)(2,1)}, u32[]{:S(2)}, u32[]{:S(2)}) async-start(bf16[32,2,128,128]{3,2,1,0:T(8,128)(2,1)} %bitcast.7), calls=%async_computation.1 | async-start | bytes 4194304 | tf_op jit(solution)/shard_map/all_to_all | solution.py:41
  54.5 2.5 copy-start.1
  54.6 2.5 copy-start.4
  54.6 2.5 copy-start.5
  114.4 55.6 %all-to-all-start.3 = ((bf16[32,2,128,128]{3,2,1,0:T(8,128)(2,1)}), bf16[32,2,128,128]{3,2,1,0:T(8,128)(2,1)}, u32[]{:S(2)}, u32[]{:S(2)}) async-start(bf16[32,2,128,128]{3,2,1,0:T(8,128)(2,1)} %bitcast.15), calls=%async_computation.4 | async-start | bytes 4194304 | tf_op jit(solution)/shard_map/all_to_all | solution.py:71
  124.1 64.8 %all-gather.3.cloned.1.call-start = ((), (), s32[]{:S(2)}) async-start(), calls=%async_computation.7 | async-start | bytes 2359296 | tf_op jit(solution)/shard_map/all_gather | solution.py:78
  174.2 14.7 %copy-start.8 = (bf16[1024,128]{1,0:T(8,128)(2,1)S(1)}, bf16[1024,128]{1,0:T(8,128)(2,1)}, u32[]{:S(2)}) copy-start(bf16[1024,128]{1,0:T(8,128)(2,1)} %param.21) | copy-start | bytes 786436
  194.0 58.5 %all-to-all-start.2 = ((bf16[32,2,128,128]{3,2,1,0:T(8,128)(2,1)}), bf16[32,2,128,128]{3,2,1,0:T(8,128)(2,1)S(1)}, u32[]{:S(2)}, u32[]{:S(2)}) async-start(bf16[32,2,128,128]{3,2,1,0:T(8,128)(2,1)} %bitcast.88), calls=%async_computation.2 | async-start | bytes 4194304 | tf_op jit(solution)/shard_map/all_to_all | solution.py:41
  203.6 111.2 %all-gather.5.cloned.1.call-start = ((), (), s32[]{:S(2)}) async-start(), calls=%async_computation.8 | async-start | bytes 2359296 | tf_op jit(solution)/shard_map/all_gather | solution.py:78
  288.7 29.5 %all-to-all-start.4 = ((f32[32,32,128]{2,1,0:T(8,128)}), f32[32,32,128]{2,1,0:T(8,128)S(1)}, u32[]{:S(2)}, u32[]{:S(2)}) async-start(f32[32,32,128]{2,1,0:T(8,128)} %bitcast.18), calls=%async_computation.5 | async-start | bytes 1048576 | tf_op jit(solution)/shard_map/all_to_all | solution.py:87
  314.9 13.5 %copy-start.3 = (bf16[1024,1024]{1,0:T(8,128)(2,1)S(1)}, bf16[1024,1024]{1,0:T(8,128)(2,1)}, u32[]{:S(2)}) copy-start(bf16[1024,1024]{1,0:T(8,128)(2,1)} %all-gather.5.cloned.1.call-done) | copy-start | bytes 6291460
  318.1 23.6 %all-to-all-start.5 = ((f32[32,32,128]{2,1,0:T(8,128)}), f32[32,32,128]{2,1,0:T(8,128)S(1)}, u32[]{:S(2)}, u32[]{:S(2)}) async-start(f32[32,32,128]{2,1,0:T(8,128)} %bitcast.19), calls=%async_computation.6 | async-start | bytes 1048576 | tf_op jit(solution)/shard_map/all_to_all | solution.py:87
Sparse Core Ops, SparseCore 0:
  11.9 41.5 reduce-scatter.1
  156.6 32.1 all-gather.2
  285.7 29.1 all-gather.4

commit v2 on v0

v2 whole, which is shorter than its diff:
```python
import jax
import jax.numpy as jnp
from jax import lax
from jax.experimental import pallas as pl
from jax.experimental.pallas import tpu as pltpu
from jax.sharding import PartitionSpec as P

MESH = pl.DeviceIdType.MESH
ROWS = 4
RING = 8
FEAT = 8
BLKS = 8
BS = 128
WIDTH = 128
GROUP = 4
F32 = jnp.float32
BF16 = jnp.bfloat16
VMEM = pl.BlockSpec(memory_space=pltpu.VMEM)
SMEM = pl.BlockSpec(memory_space=pltpu.SMEM)
DMA = pltpu.SemaphoreType.DMA


def whereabouts():
    node, feat = lax.axis_index("nodes"), lax.axis_index("feat")
    return lax.div(node, RING), lax.rem(node, RING), feat


def node_at(y, z, dy, dz):
    return lax.rem(y + dy + ROWS, ROWS) * RING + lax.rem(z + dz + RING, RING)


def feat_at(f, dx, dc):
    core = lax.rem(f, 2)
    chip = lax.div(f, 2)
    return lax.rem(chip + dx, 4) * 2 + lax.rem(core + dc, 2)


def greet(partners):
    barrier = pltpu.get_barrier_semaphore()
    for partner in partners:
        pl.semaphore_signal(barrier, inc=1, device_id=partner, device_id_type=MESH)
    pl.semaphore_wait(barrier, len(partners))


def send(src, dst, send_sem, recv_sem, device):
    return pltpu.make_async_remote_copy(
        src_ref=src,
        dst_ref=dst,
        send_sem=send_sem,
        recv_sem=recv_sem,
        device_id=device,
        device_id_type=MESH,
    )


FROM_BELOW = [(7, 0), (7, 1), (6, 0), (6, 1), (5, 0), (5, 1), (4, 0)]
FROM_ABOVE = [(1, 0), (1, 1), (2, 0), (2, 1), (3, 0), (3, 1), (4, 1)]


def gather_scratch():
    return [pltpu.VMEM((BLKS, BS, WIDTH), BF16)] * 7 + [
        pltpu.VMEM((RING, 3, 2, BS, WIDTH), BF16),
        DMA((2, 7)),
        DMA((2, 7)),
        DMA((RING, 3)),
        DMA((RING, 3)),
    ]


def gather_stages(place, field, table, ghost, scratch):
    y, z, f = place
    chunks = [field] + list(scratch[:7])
    picked, zs, zr, ys, yr = scratch[7:]
    above, below = (node_at(y, z, 0, 1), f), (node_at(y, z, 0, -1), f)

    def half(ref, h):
        return ref.at[pl.ds(4 * h, 4)]

    up, down = [], []
    for i in range(7):
        o, h = FROM_BELOW[i]
        up.append(
            send(half(chunks[(o + 1) % 8], h), half(chunks[o], h), zs.at[0, i], zr.at[0, i], above)
        )
        o, h = FROM_ABOVE[i]
        down.append(
            send(half(chunks[o - 1], h), half(chunks[o], h), zs.at[1, i], zr.at[1, i], below)
        )
    across = []

    def deal(o):
        zz = lax.rem(z + o, RING)
        base = (y * RING + zz) * 2
        chunk = chunks[o]
        for dy in (1, 3, 2):
            reader = lax.rem(y + dy, ROWS)
            for j in range(2):
                picked[o, dy - 1, j] = chunk[table[reader, zz, j]]
            copy = send(
                picked.at[o, dy - 1],
                ghost.at[pl.ds(base, 2)],
                ys.at[o, dy - 1],
                yr.at[o, dy - 1],
                (node_at(y, z, dy, 0), f),
            )
            copy.start()
            across.append(copy)
        for j in range(2):
            ghost[base + j] = chunk[table[y, zz, j]]

    for i in range(2):
        up[i].start()
        down[i].start()
    yield
    deal(0)
    yield
    for i in range(7):
        up[i].wait_recv()
        if i + 2 < 7:
            up[i + 2].start()
        down[i].wait_recv()
        if i + 2 < 6:
            down[i + 2].start()
        if i == 5:
            down[6].start()
        if i in (1, 3, 5):
            deal(FROM_BELOW[i][0])
            deal(FROM_ABOVE[i][0])
        if i == 6:
            deal(4)
        yield
    for copy in across:
        copy.wait()
    for copy in up + down:
        copy.wait_send()
    yield


def run(*stage_lists):
    live = list(stage_lists)
    while live:
        for stages in list(live):
            try:
                next(stages)
            except StopIteration:
                live.remove(stages)


def first_kernel(field, wants, weight_two, ghost, requests, two_rows, *scratch):
    place = y, z, f = whereabouts()
    table, ts, tr, ws, wr, local = scratch[:6]
    rest = scratch[6:]
    cols = [(node_at(y, z, dy, 0), f) for dy in (1, 2, 3)]
    ring = [(node_at(y, z, 0, 1), f), (node_at(y, z, 0, -1), f)]
    wide = [(lax.axis_index("nodes"), lax.rem(f + d, FEAT)) for d in range(1, FEAT)]
    greet(cols + ring + wide)
    asks = []
    for dy in (1, 2, 3):
        copy = send(
            wants.at[lax.rem(y + dy, ROWS)],
            requests.at[y],
            ts.at[dy - 1],
            tr.at[dy - 1],
            cols[dy - 1],
        )
        copy.start()
        asks.append(copy)
    stages = gather_stages(place, field, table, ghost, rest)
    next(stages)
    parts = []
    for d in range(1, FEAT):
        copy = send(
            weight_two.at[lax.rem(f + d, FEAT)],
            two_rows.at[f],
            ws.at[d - 1],
            wr.at[d - 1],
            wide[d - 1],
        )
        copy.start()
        parts.append(copy)
    two_rows[f] = weight_two[f]
    requests[y] = wants[y]
    for copy in asks:
        copy.wait_recv()
    move = pltpu.make_async_copy(requests, table, local)
    move.start()
    move.wait()
    run(stages)
    for copy in asks:
        copy.wait_send()
    for copy in parts:
        copy.wait()


def fetch_first(field, wants, weight_two):
    return pl.pallas_call(
        first_kernel,
        out_shape=(
            jax.ShapeDtypeStruct((2 * ROWS * RING, BS, WIDTH), BF16),
            jax.ShapeDtypeStruct((ROWS, RING, 128), jnp.int32),
            jax.ShapeDtypeStruct((FEAT, 128, WIDTH), BF16),
        ),
        in_specs=[VMEM] * 3,
        out_specs=(VMEM,) * 3,
        scratch_shapes=[
            pltpu.SMEM((ROWS, RING, 128), jnp.int32),
            DMA((3,)),
            DMA((3,)),
            DMA((7,)),
            DMA((7,)),
            DMA(()),
        ]
        + gather_scratch(),
        compiler_params=pltpu.CompilerParams(collective_id=0, has_side_effects=True),
    )(field, wants, weight_two)


def spread_rows(steps, slots, tiles, shares, field, ghost, table, out):
    @pl.loop(0, BLKS)
    def _(r):
        def advance(t, total):
            first = t * GROUP
            left = jnp.concatenate([table[tiles[r, first + g]] for g in range(GROUP)], axis=1)
            right = jnp.concatenate([ghost[slots[r, first + g]] for g in range(GROUP)], axis=0)
            return total + jnp.dot(left, right, preferred_element_type=F32)

        total = lax.fori_loop(0, steps[r], advance, jnp.zeros((BS, WIDTH), F32))
        out[r] = (field[r].astype(F32) + shares[r] * total).astype(out.dtype)


def share_rows(steps, slots, tiles, shares, field, turned, totals, out):
    @pl.loop(0, 64)
    def _(s):
        totals[s] = jnp.zeros((BS, WIDTH), F32)

    @pl.loop(0, BLKS)
    def _(r):
        block = field[r]

        def advance(t, carry):
            first = t * GROUP
            left = jnp.concatenate([turned[tiles[r, first + g]] for g in range(GROUP)], axis=0)
            terms = shares[r] * jnp.dot(left, block, preferred_element_type=F32)
            for g in range(GROUP):
                totals[slots[r, first + g]] += terms[g * BS : (g + 1) * BS]
            return carry

        lax.fori_loop(0, steps[r], advance, 0)

    @pl.loop(0, 64)
    def _(s):
        out[s] = totals[s].astype(BF16)


def local_kernel(steps, slots, tiles, shares, field, ghost, cot, table, out, partial, turned, totals):
    @pl.loop(0, 17)
    def _(t):
        turned[t] = table[t].T

    share_rows(steps, slots, tiles, shares, cot, turned, totals, partial)
    spread_rows(steps, slots, tiles, shares, field, ghost, table, out)


def spread_both(plan, field, ghost, cot, table):
    return pl.pallas_call(
        local_kernel,
        out_shape=(
            jax.ShapeDtypeStruct((BLKS, BS, WIDTH), BF16),
            jax.ShapeDtypeStruct((64, BS, WIDTH), BF16),
        ),
        in_specs=[SMEM] * 4 + [VMEM] * 4,
        out_specs=(VMEM,) * 2,
        scratch_shapes=[
            pltpu.VMEM((17, BS, BS), BF16),
            pltpu.VMEM((64, BS, WIDTH), F32),
        ],
    )(*plan, field, ghost, cot, table)


def spread_one(plan, field, ghost, table):
    return pl.pallas_call(
        spread_rows,
        out_shape=jax.ShapeDtypeStruct((BLKS, BS, WIDTH), BF16),
        in_specs=[SMEM] * 4 + [VMEM] * 3,
        out_specs=VMEM,
    )(*plan, field, ghost, table)


def widen_scratch():
    return [DMA((4,)), DMA((4,)), DMA((4,)), DMA((4,))]


def widen_stages(place, own, wide, scratch):
    y, z, f = place
    node = lax.axis_index("nodes")
    xs, xr, cs, cr = scratch
    twin = (node, feat_at(f, 0, 1))
    far = []
    for i, dx in enumerate((1, 3, 2)):
        copy = send(own, wide.at[f], xs.at[i], xr.at[i], (node, feat_at(f, dx, 0)))
        copy.start()
        far.append(copy)
    near = []
    for i, dx in enumerate((0, 3, 1, 2)):
        source = feat_at(f, dx, 0)
        if i > 0:
            far[i - 1].wait_recv()
        block = wide.at[source] if i > 0 else own
        copy = send(block, wide.at[source], cs.at[i], cr.at[i], twin)
        copy.start()
        near.append(copy)
        yield
    for copy in near:
        copy.wait_recv()
    for copy in near + far:
        copy.wait_send()
    yield


def widen_partners(place):
    node = lax.axis_index("nodes")
    f = place[2]
    return [(node, feat_at(f, dx, 0)) for dx in (1, 2, 3)] + [(node, feat_at(f, 0, 1))]


TO_ABOVE = [(4, 0), (3, 0), (3, 1), (2, 0), (2, 1), (1, 0), (1, 1)]
TO_BELOW = [(4, 1), (5, 1), (5, 0), (6, 1), (6, 0), (7, 1), (7, 0)]


def settle_scratch():
    return [
        pltpu.VMEM((RING, 3, 2, BS, WIDTH), BF16),
        pltpu.VMEM((RING, BLKS, BS, WIDTH), BF16),
        pltpu.VMEM((2, 7, 4, BS, WIDTH), BF16),
        DMA((RING, 3)),
        DMA((RING, 3)),
        DMA((2, 7)),
        DMA((2, 7)),
    ]


def settle_stages(place, partial, table, own, out, scratch):
    y, z, f = place
    landed, held, came, ys, yr, zs, zr = scratch
    above, below = (node_at(y, z, 0, 1), f), (node_at(y, z, 0, -1), f)
    order = (4, 3, 5, 2, 6, 1, 7, 0)
    across = {}
    for o in order:
        zz = lax.rem(z + o, RING)
        for dy in (1, 3, 2):
            owner = lax.rem(y + dy, ROWS)
            copy = send(
                partial.at[pl.ds((owner * RING + zz) * 2, 2)],
                landed.at[o, dy - 1],
                ys.at[o, dy - 1],
                yr.at[o, dy - 1],
                (node_at(y, z, dy, 0), f),
            )
            copy.start()
            across[o, dy] = copy
    yield

    def gathered(o, h, extras, base, store):
        zz = lax.rem(z + o, RING)
        sources, where = [], []
        for dy in range(ROWS):
            reader = lax.rem(y + ROWS - dy, ROWS)
            for j in range(2):
                where.append(table[reader, zz, j])
                sources.append((dy, j))
        marks = [
            [jnp.where(where[i] == 4 * h + b, 1.0, 0.0).astype(F32) for i in range(8)]
            for b in range(4)
        ]
        first = (y * RING + zz) * 2

        @pl.loop(0, BS // 16)
        def _(t):
            rows = pl.ds(pl.multiple_of(t * 16, 16), 16)
            values = []
            for dy, j in sources:
                if dy == 0:
                    value = partial[first + j, rows, :]
                else:
                    value = landed[o, dy - 1, j, rows, :]
                values.append(value.astype(F32))
            for b in range(4):
                total = marks[b][0] * values[0]
                for i in range(1, 8):
                    total = total + marks[b][i] * values[i]
                for lane, index in extras:
                    total = total + came[lane, index, b, rows, :].astype(F32)
                if base is not None:
                    total = total + base[4 * h + b, rows, :].astype(F32)
                store[4 * h + b, rows, :] = total.astype(BF16)

    def piece(lane, index, o, h):
        return send(
            held.at[o, pl.ds(4 * h, 4)],
            came.at[lane, index],
            zs.at[lane, index],
            zr.at[lane, index],
            above if lane == 0 else below,
        )

    def feeds(lane, o, h):
        lists = (TO_ABOVE, TO_BELOW)
        step = 1 if lane == 0 else -1
        source = (o + step) % 8
        return [(lane, i) for i, item in enumerate(lists[lane]) if item == (source, h)]

    pieces = {}

    def land(o):
        for dy in (1, 2, 3):
            across[o, dy].wait_recv()

    def forward(lane, index):
        o, h = (TO_ABOVE, TO_BELOW)[lane][index]
        extras = feeds(lane, o, h)
        for key in extras:
            pieces[key].wait_recv()
        gathered(o, h, extras, None, held.at[o])
        pieces[lane, index] = piece(lane, index, o, h)
        pieces[lane, index].start()

    land(4)
    forward(0, 0)
    forward(1, 0)
    yield
    for step, (a, b) in enumerate(((3, 5), (2, 6), (1, 7))):
        land(a)
        land(b)
        for half in range(2):
            forward(0, 1 + 2 * step + half)
            forward(1, 1 + 2 * step + half)
            yield
    land(0)
    for half in range(2):
        extras = feeds(0, 0, half) + feeds(1, 0, half)
        for key in extras:
            pieces[key].wait_recv()
        gathered(0, half, extras, own, out)
        yield
    for copy in list(across.values()) + list(pieces.values()):
        copy.wait_send()
    yield


def column(y, z, f):
    return [(node_at(y, z, dy, 0), f) for dy in (1, 2, 3)]


def times(wide, weight, rows):
    total = None
    for pair in range(FEAT // 2):
        left = jnp.concatenate([wide[2 * pair, rows, :], wide[2 * pair + 1, rows, :]], axis=1)
        right = jnp.concatenate([weight[2 * pair], weight[2 * pair + 1]], axis=0)
        term = jnp.dot(left, right, preferred_element_type=F32)
        total = term if total is None else total + term
    return total


TILE = 256


def second_kernel(
    table,
    agg,
    partial,
    cot,
    weight_one,
    weight_two,
    agg_wide,
    hidden_wide,
    pre_one,
    mixed,
    back,
    *scratch,
):
    place = y, z, f = whereabouts()
    ring = [(node_at(y, z, 0, 1), f), (node_at(y, z, 0, -1), f)]
    greet(column(y, z, f) + ring + widen_partners(place))
    agg_wide[f] = agg[...]
    first = widen_stages(place, agg, agg_wide, scratch[:4])
    settle = settle_stages(place, partial, table, cot, back, scratch[8:])
    next(first)
    next(settle)
    next(first)
    next(settle)
    next(first)
    next(settle)
    run(first)

    @pl.loop(0, 1024 // TILE)
    def _(t):
        rows = pl.ds(pl.multiple_of(t * TILE, TILE), TILE)
        pre = times(agg_wide, weight_one, rows)
        pre_one[rows, :] = pre
        hidden_wide[f, rows, :] = (pre * jax.nn.sigmoid(pre)).astype(BF16)

    second = widen_stages(place, hidden_wide.at[f], hidden_wide, scratch[4:8])
    next(second)
    next(settle)
    next(settle)
    next(second)
    next(settle)
    next(second)
    next(settle)
    run(second)

    @pl.loop(0, 1024 // TILE)
    def _(t):
        rows = pl.ds(pl.multiple_of(t * TILE, TILE), TILE)
        mixed[rows, :] = times(hidden_wide, weight_two, rows).astype(BF16)

    run(settle)


def middle(table, agg, partial, cot, weight_one, weight_two):
    wide = jax.ShapeDtypeStruct((FEAT, 1024, WIDTH), BF16)
    return pl.pallas_call(
        second_kernel,
        out_shape=(
            wide,
            wide,
            jax.ShapeDtypeStruct((1024, WIDTH), F32),
            jax.ShapeDtypeStruct((1024, WIDTH), BF16),
            jax.ShapeDtypeStruct((BLKS, BS, WIDTH), BF16),
        ),
        in_specs=[SMEM] + [VMEM] * 5,
        out_specs=(VMEM,) * 5,
        scratch_shapes=widen_scratch() + widen_scratch() + settle_scratch(),
        compiler_params=pltpu.CompilerParams(collective_id=1, has_side_effects=True),
    )(table, agg, partial, cot, weight_one, weight_two)


def reduce_scratch():
    return [
        pltpu.VMEM((ROWS, 256, WIDTH), F32),
        pltpu.VMEM((3, 256, WIDTH), F32),
        pltpu.VMEM((RING, 32, WIDTH), F32),
        pltpu.VMEM((7, 32, WIDTH), F32),
        DMA((3,)),
        DMA((3,)),
        DMA((7,)),
        DMA((7,)),
    ]


def reduce_stages(place, out, scratch):
    y, z, f = place
    shares, came, mine, landed, ys, yr, zs, zr = scratch
    across = []
    for dy in (1, 3, 2):
        copy = send(
            shares.at[lax.rem(y + dy, ROWS)],
            came.at[dy - 1],
            ys.at[dy - 1],
            yr.at[dy - 1],
            (node_at(y, z, dy, 0), f),
        )
        copy.start()
        across.append(copy)
    yield
    for copy in across:
        copy.wait_recv()
    for o in range(RING):
        rows = pl.ds(o * 32, 32)
        mine[o] = shares[y, rows, :] + came[0, rows, :] + came[1, rows, :] + came[2, rows, :]
    along = []
    for dz in (4, 3, 5, 2, 6, 1, 7):
        copy = send(
            mine.at[lax.rem(z + dz, RING)],
            landed.at[dz - 1],
            zs.at[dz - 1],
            zr.at[dz - 1],
            (node_at(y, z, 0, dz), f),
        )
        copy.start()
        along.append(copy)
    yield
    for copy in along:
        copy.wait_recv()
    total = mine[z]
    for i in range(7):
        total = total + landed[i]
    out[...] = total
    for copy in across + along:
        copy.wait_send()
    yield


def outer(wide, right, shares):
    @pl.loop(0, ROWS)
    def _(i):
        for j in range(2):
            shares[i, pl.ds(j * 128, 128), :] = lax.dot_general(
                wide[2 * i + j], right[...], (((0,), (0,)), ((), ())), preferred_element_type=F32
            )


def third_kernel(
    table,
    mixed,
    back,
    agg_wide,
    hidden_wide,
    pre_one,
    two_rows,
    ghost,
    grad_one,
    grad_two,
    back_wide,
    back_pre,
    back_flat,
    *scratch,
):
    place = y, z, f = whereabouts()
    along = [(node_at(y, z, 0, dz), f) for dz in range(1, RING)]
    greet(column(y, z, f) + along + widen_partners(place))
    gather = gather_stages(place, mixed, table, ghost, scratch[:12])
    next(gather)
    back_wide[f] = back[...].reshape(1024, WIDTH)
    widen = widen_stages(place, back_wide.at[f], back_wide, scratch[12:16])
    next(widen)
    next(gather)
    back_flat[...] = back[...].reshape(1024, WIDTH)
    next(widen)
    outer(hidden_wide, back_flat, scratch[24])
    next(gather)
    next(gather)
    two = reduce_stages(place, grad_two, scratch[24:32])
    next(two)
    next(widen)
    next(gather)
    next(widen)
    next(gather)
    run(widen)

    @pl.loop(0, 1024 // TILE)
    def _(t):
        rows = pl.ds(pl.multiple_of(t * TILE, TILE), TILE)
        total = None
        for pair in range(FEAT // 2):
            left = jnp.concatenate(
                [back_wide[2 * pair, rows, :], back_wide[2 * pair + 1, rows, :]], axis=1
            )
            right = jnp.concatenate([two_rows[2 * pair], two_rows[2 * pair + 1]], axis=1)
            term = lax.dot_general(
                left, right, (((1,), (1,)), ((), ())), preferred_element_type=F32
            )
            total = term if total is None else total + term
        pre = pre_one[rows, :]
        sigma = jax.nn.sigmoid(pre)
        back_pre[rows, :] = (total * sigma * (1.0 + pre * (1.0 - sigma))).astype(BF16)

    next(gather)
    outer(agg_wide, back_pre, scratch[16])
    one = reduce_stages(place, grad_one, scratch[16:24])
    next(one)
    next(gather)
    next(two)
    next(gather)
    next(one)
    run(gather, two, one)


def last(table, mixed, back, agg_wide, hidden_wide, pre_one, two_rows):
    return pl.pallas_call(
        third_kernel,
        out_shape=(
            jax.ShapeDtypeStruct((2 * ROWS * RING, BS, WIDTH), BF16),
            jax.ShapeDtypeStruct((32, WIDTH), F32),
            jax.ShapeDtypeStruct((32, WIDTH), F32),
        ),
        in_specs=[SMEM] + [VMEM] * 6,
        out_specs=(VMEM,) * 3,
        scratch_shapes=[
            pltpu.VMEM((FEAT, 1024, WIDTH), BF16),
            pltpu.VMEM((1024, WIDTH), BF16),
            pltpu.VMEM((1024, WIDTH), BF16),
        ]
        + gather_scratch()
        + widen_scratch()
        + reduce_scratch()
        + reduce_scratch(),
        compiler_params=pltpu.CompilerParams(collective_id=2, has_side_effects=True),
    )(table, mixed, back, agg_wide, hidden_wide, pre_one, two_rows)


def on_device(
    features, ghosts, slots, tile_ids, degrees, tile_table, weight_one, weight_two, cotangent
):
    blocks = features.reshape(BLKS, BS, WIDTH)
    cot = cotangent.reshape(BLKS, BS, WIDTH)
    wants = jnp.pad(ghosts.reshape(ROWS, RING, 2), ((0, 0), (0, 0), (0, 126)))
    position = lax.broadcasted_iota(jnp.int32, slots.shape, 1)
    live_tiles = jnp.where(position < degrees[:, None], tile_ids, 16)
    steps = (degrees + GROUP - 1) // GROUP
    plan = (steps, slots, live_tiles, lax.rsqrt(degrees.astype(F32)))
    table = jnp.pad(tile_table, ((0, 1), (0, 0), (0, 0)))
    one = weight_one.reshape(FEAT, 128, WIDTH)
    two = weight_two.reshape(FEAT, 128, WIDTH)
    ghost, requests, two_rows = fetch_first(blocks, wants, two)
    agg, partial = spread_both(plan, blocks, ghost, cot, table)
    agg_wide, hidden_wide, pre_one, mixed, back = middle(
        requests, agg.reshape(1024, WIDTH), partial, cot, one, two
    )
    mixed = mixed.reshape(BLKS, BS, WIDTH)
    ghost_two, grad_one, grad_two = last(
        requests, mixed, back, agg_wide, hidden_wide, pre_one, two_rows
    )
    output = spread_one(plan, mixed, ghost_two, table)
    return (output.reshape(1024, WIDTH), grad_one, grad_two)


def solution(mesh):
    return jax.shard_map(
        on_device,
        mesh=mesh,
        in_specs=(
            P("nodes", "feat"),
            P("nodes", None),
            P("nodes", None),
            P("nodes", None),
            P("nodes"),
            P(),
            P(None, "feat"),
            P(None, "feat"),
            P("nodes", "feat"),
        ),
        out_specs=(P("nodes", "feat"), P("nodes", "feat"), P("nodes", "feat")),
        check_vma=False,
    )
```

time: 756 us -> 173 us (0.23)
  waiting for transfers between devices: 530 us -> 0 us
  Pallas kernels: 0 us -> 162 us
  other arithmetic: 76.2 us -> 3.72 us
  matrix products: 44.1 us -> 0 us
  local copies, waits for them, and re-layouts: 41.3 us -> 4.51 us
  starting transfers between devices: 24.3 us -> 0 us
  blocking collectives: 20.5 us -> 0 us
  between operations: 14 us -> 0.67 us
    reduce_scatter x3 -> x0, waiting for transfers between devices: 437 us -> none  [the longest x2 424 us: weight_grad(): lax.psum_scatter(lax.dot_general(wide_rows, local_rows, (((0,), (0,)), ((...]
    pallas_call x0 -> x5, Pallas kernels: none -> 162 us  [the longest x1 52.1 us: middle(): pl.pallas_call(second_kernel, out_shape=(wide, wide, jax.ShapeDtypeStruct...]
    all_to_all x3 -> x0, waiting for transfers between devices: 60.8 us -> none  [the longest x2 48.7 us: neighbours(): lax.all_to_all(outgoing, 'nodes', split_axis=0, concat_axis=0, tiled=True)]
    scatter-add x4 -> x0, other arithmetic: 49.8 us -> none  [the longest x3 41 us: scatter_advance(): jax.ops.segment_sum(scaled.reshape(-1, block_size, feat_width), near_ids....]
    dot_general x14 -> x0, matrix products: 44.1 us -> none  [the longest x6 20.7 us: collect_advance(): jnp.einsum('bkij,bkjf->bkif', picked, near_rows, preferred_element_type=j...]
    gather x17 -> x0, local copies, waits for them, and re-layouts: 34.1 us -> none  [the longest x6 17.6 us: collect_advance(): near_rows = ghost_rows[near_ids]]
    all_gather x2 -> x0, waiting for transfers between devices: 31.9 us -> none  [widen(): return lax.all_gather(values, 'feat', axis=1, tiled=True)]
    all_to_all x3 -> x0, starting transfers between devices: 24 us -> none  [the longest x2 14.5 us: neighbours(): lax.all_to_all(outgoing, 'nodes', split_axis=0, concat_axis=0, tiled=True)]
  transfers between devices with their start and end apart: 8 -> 0, of which waited for: 7 -> 0; matrix products, arithmetic and copies ran while one was open for 16% -> 0% of each run, Pallas kernels for 0% -> 0%
where the time goes in v2:
time: 173 us; the launch traced here: 171 us
  Pallas kernels  162 us (94%)
  local copies, waits for them, and re-layouts  4.51 us (3%)
  other arithmetic  3.72 us (2%)
    pallas_call x1, Pallas kernels, middle(): pl.pallas_call(second_kernel, out_shape=(wide, wide, jax.ShapeDtypeStruct...  52.1 us
    pallas_call x1, Pallas kernels, last(): pl.pallas_call(third_kernel, out_shape=(jax.ShapeDtypeStruct((2 * ROWS *...  49.7 us
    pallas_call x1, Pallas kernels, fetch_first(): pl.pallas_call(first_kernel, out_shape=(jax.ShapeDtypeStruct((2 * ROWS *...  42 us
    pallas_call x1, Pallas kernels, spread_both(): pl.pallas_call(local_kernel, out_shape=(jax.ShapeDtypeStruct((BLKS, BS, W...  12.5 us
    pallas_call x1, Pallas kernels, spread_one(): pl.pallas_call(spread_rows, out_shape=jax.ShapeDtypeStruct((BLKS, BS, WID...  6.13 us

profile of v2, /device:TPU:1, one launch (start us, length us, event | category | flops | bytes accessed | tf_op | source)
XLA Modules:
  0.0 171.3 jit_solution(17575487780479638795)
XLA Ops:
  0.6 1.2 and_select_fusion.steps
  1.8 1.2 convert_rsqrt_fusion.shares
  3.0 1.4 fusion.tiles
  4.4 0.8 copy.13
  5.1 0.6 pad.8.wants
  5.7 1.9 %pad.9.table = bf16[17,128,128]{2,1,0:T(8,128)(2,1)} pad(bf16[16,128,128]{2,1,0:T(8,128)(2,1)} %param.14, bf16[]{:T(256)} %constant.24.clone.1), padding=0_1x0_0x0_0 | pad | bytes 1081346 | tf_op jit(solution)/shard_map/jit(_pad)/pad | solution.py:702
  7.6 42.0 %shard_map.112 = (bf16[64,128,128]{2,1,0:T(8,128)(2,1)}, s32[4,8,128]{2,1,0:T(8,128)}, bf16[8,128,128]{2,1,0:T(8,128)(2,1)}) custom-call(bf16[8,128,128]{2,1,0:T(8,128)(2,1)} %bitcast.10, s32[4,8,128]{2,1,0:T(8,128)} %pad.8.wants, bf16[8,128,128]{2,1,0:T(8,128)(2,1)} %bitcast.12), custom_call_target="tpu_custom_call" | custom-call | tf_op jit(solution)/shard_map/pallas_call | solution.py:196
  49.6 12.5 %shard_map.113 = (bf16[8,128,128]{2,1,0:T(8,128)(2,1)}, bf16[64,128,128]{2,1,0:T(8,128)(2,1)}) custom-call(s32[8]{0:T(128)} %and_select_fusion.steps, s32[8,24]{1,0:T(8,128)} %slots.3, s32[8,24]{1,0:T(8,128)} %fusion.tiles, f32[8]{0:T(128)} %convert_rsqrt_fusion.shares, bf16[8,128,128]{2,1,0:T(8,128)(2,1)} %bitcast.11, ...), custom_call_target="tpu_custom_call" | custom-call | tf_op jit(solution)/shard_map/pallas_call | solution.py:265
  62.1 52.1 %shard_map.114 = (bf16[8,1024,128]{2,1,0:T(8,128)(2,1)}, bf16[8,1024,128]{2,1,0:T(8,128)(2,1)}, f32[1024,128]{1,0:T(8,128)}, bf16[1024,128]{1,0:T(8,128)(2,1)}, bf16[8,128,128]{2,1,0:T(8,128)(2,1)}) custom-call(s32[4,8,128]{2,1,0:T(8,128)} %get-tuple-element.16.table, bf16[1024,128]{1,0:T(8,128)(2,1)} %bitcast.18, ...), custom_call_target="tpu_custom_call" | custom-call | tf_op jit(solution)/shard_map/pallas_call | solution.py:522
  114.2 49.7 %shard_map.115 = (bf16[64,128,128]{2,1,0:T(8,128)(2,1)}, f32[32,128]{1,0:T(8,128)}, f32[32,128]{1,0:T(8,128)}) custom-call(s32[4,8,128]{2,1,0:T(8,128)} %get-tuple-element.16.table, bf16[8,128,128]{2,1,0:T(8,128)(2,1)} %bitcast.14, bf16[8,128,128]{2,1,0:T(8,128)(2,1)} %get-tuple-element.21.back, bf16[8,1024,128]{2,1,0:T(8,128)(2,1)} %get-tuple-element.22.agg_wide, ...), custom_call_target="tpu_custom_call" | custom-call | tf_op jit(solution)/shard_map/pallas_call | solution.py:670
  163.9 0.0 copy-start.1
  163.9 0.0 copy-start
  163.9 6.1 %shard_map.116 = bf16[8,128,128]{2,1,0:T(8,128)(2,1)} custom-call(s32[8]{0:T(128)} %and_select_fusion.steps, s32[8,24]{1,0:T(8,128)} %slots.3, s32[8,24]{1,0:T(8,128)} %fusion.tiles, f32[8]{0:T(128)} %convert_rsqrt_fusion.shares, bf16[8,128,128]{2,1,0:T(8,128)(2,1)} %bitcast.15, bf16[64,128,128]{2,1,0:T(8,128)(2,1)} %get-tuple-element.26.ghost, ...), custom_call_target="tpu_custom_call" | custom-call | tf_op jit(solution)/shard_map/pallas_call | solution.py:281
  170.1 0.0 copy-done.1
  170.1 0.6 copy.16
  170.7 0.0 copy-done
  170.7 0.6 copy.17
Async XLA Ops:
  163.9 6.2 %copy-start.1 = (f32[32,128]{1,0:T(8,128)S(1)}, f32[32,128]{1,0:T(8,128)}, u32[]{:S(2)}) copy-start(f32[32,128]{1,0:T(8,128)} %get-tuple-element.33) | copy-start | bytes 49156
  163.9 6.8 %copy-start = (f32[32,128]{1,0:T(8,128)S(1)}, f32[32,128]{1,0:T(8,128)}, u32[]{:S(2)}) copy-start(f32[32,128]{1,0:T(8,128)} %get-tuple-element.34) | copy-start | bytes 49156

commit v3 on v2

v3 whole, which is shorter than its diff:
```python
import jax
import jax.numpy as jnp
from jax import lax
from jax.experimental import pallas as pl
from jax.experimental.pallas import tpu as pltpu
from jax.sharding import PartitionSpec as P

MESH = pl.DeviceIdType.MESH
ROWS = 4
RING = 8
FEAT = 8
BLKS = 8
BS = 128
WIDTH = 128
GROUP = 4
DEPTH = 24
PART = 256
PARTS = 4
F32 = jnp.float32
BF16 = jnp.bfloat16
VMEM = pl.BlockSpec(memory_space=pltpu.VMEM)
SMEM = pl.BlockSpec(memory_space=pltpu.SMEM)
DMA = pltpu.SemaphoreType.DMA


def whereabouts():
    node, feat = lax.axis_index("nodes"), lax.axis_index("feat")
    return lax.div(node, RING), lax.rem(node, RING), feat


def node_at(y, z, dy, dz):
    return lax.rem(y + dy + ROWS, ROWS) * RING + lax.rem(z + dz + RING, RING)


def feat_at(f, dx, dc):
    core = lax.rem(f, 2)
    chip = lax.div(f, 2)
    return lax.rem(chip + dx, 4) * 2 + lax.rem(core + dc, 2)


def greet(partners):
    barrier = pltpu.get_barrier_semaphore()
    for partner in partners:
        pl.semaphore_signal(barrier, inc=1, device_id=partner, device_id_type=MESH)
    pl.semaphore_wait(barrier, len(partners))


def send(src, dst, send_sem, recv_sem, device):
    return pltpu.make_async_remote_copy(
        src_ref=src,
        dst_ref=dst,
        send_sem=send_sem,
        recv_sem=recv_sem,
        device_id=device,
        device_id_type=MESH,
    )


def wanted(table, y, reader, j, zz):
    return table[reader, j, y * RING + zz]


FROM_BELOW = [(7, 0), (7, 1), (6, 0), (6, 1), (5, 0), (5, 1), (4, 0)]
FROM_ABOVE = [(1, 0), (1, 1), (2, 0), (2, 1), (3, 0), (3, 1), (4, 1)]


def gather_scratch():
    return [pltpu.VMEM((BLKS, BS, WIDTH), BF16)] * 7 + [
        pltpu.VMEM((RING, 3, 2, BS, WIDTH), BF16),
        pltpu.VMEM((2 * ROWS * RING, BS, WIDTH), BF16),
        DMA((2, 7)),
        DMA((2, 7)),
        DMA((RING, 3)),
        DMA((RING, 3)),
    ]


def gather_stages(place, field, table, scratch):
    y, z, f = place
    chunks = [field] + list(scratch[:7])
    picked, ghost, zs, zr, ys, yr = scratch[7:]
    above, below = (node_at(y, z, 0, 1), f), (node_at(y, z, 0, -1), f)

    def half(ref, h):
        return ref.at[pl.ds(4 * h, 4)]

    up, down = [], []
    for i in range(7):
        o, h = FROM_BELOW[i]
        up.append(
            send(half(chunks[(o + 1) % 8], h), half(chunks[o], h), zs.at[0, i], zr.at[0, i], above)
        )
        o, h = FROM_ABOVE[i]
        down.append(
            send(half(chunks[o - 1], h), half(chunks[o], h), zs.at[1, i], zr.at[1, i], below)
        )
    across = []

    def deal(o):
        zz = lax.rem(z + o, RING)
        base = (y * RING + zz) * 2
        chunk = chunks[o]
        for dy in (1, 3, 2):
            reader = lax.rem(y + dy, ROWS)
            for j in range(2):
                picked[o, dy - 1, j] = chunk[wanted(table, y, reader, j, zz)]
            copy = send(
                picked.at[o, dy - 1],
                ghost.at[pl.ds(base, 2)],
                ys.at[o, dy - 1],
                yr.at[o, dy - 1],
                (node_at(y, z, dy, 0), f),
            )
            copy.start()
            across.append(copy)
        for j in range(2):
            ghost[base + j] = chunk[wanted(table, y, y, j, zz)]

    for i in range(2):
        up[i].start()
        down[i].start()
        yield
    deal(0)
    yield
    for i in range(7):
        up[i].wait_recv()
        if i + 2 < 7:
            up[i + 2].start()
        down[i].wait_recv()
        if i + 2 < 6:
            down[i + 2].start()
        if i == 5:
            down[6].start()
        if i in (1, 3, 5):
            deal(FROM_BELOW[i][0])
            deal(FROM_ABOVE[i][0])
        if i == 6:
            deal(4)
        yield
    for copy in across:
        copy.wait()
    for copy in up + down:
        copy.wait_send()
    yield


def step(*stage_lists):
    for stages in stage_lists:
        next(stages, None)


def drain(stages):
    for _ in stages:
        pass


def share_kernel(degrees, slots, tiles, cot, table, out, turned, totals):
    for t in range(16):
        turned[t] = table[t].T
    turned[16] = jnp.zeros((BS, BS), BF16)

    @pl.loop(0, 64)
    def _(s):
        totals[s] = jnp.zeros((BS, WIDTH), F32)

    @pl.loop(0, BLKS)
    def _(r):
        block = cot[r]
        degree = degrees[r]
        share = lax.rsqrt(jnp.full((1, WIDTH), degree.astype(F32)))

        def advance(t, carry):
            first = t * GROUP
            picks = [
                turned[jnp.where(first + g < degree, tiles[r, first + g], 16)] for g in range(GROUP)
            ]
            terms = share * jnp.dot(
                jnp.concatenate(picks, axis=0), block, preferred_element_type=F32
            )
            for g in range(GROUP):
                totals[slots[r, first + g]] += terms[g * BS : (g + 1) * BS]
            return carry

        lax.fori_loop(0, lax.div(degree + GROUP - 1, GROUP), advance, 0)

    @pl.loop(0, 64)
    def _(s):
        out[s] = totals[s].astype(BF16)


def share_out(degrees, slots, tiles, cot, table):
    return pl.pallas_call(
        share_kernel,
        out_shape=jax.ShapeDtypeStruct((64, BS, WIDTH), BF16),
        in_specs=[SMEM] * 3 + [VMEM] * 2,
        out_specs=VMEM,
        scratch_shapes=[
            pltpu.VMEM((17, BS, BS), BF16),
            pltpu.VMEM((64, BS, WIDTH), F32),
        ],
    )(degrees, slots, tiles, cot, table)


def spread_rows(first, last, degrees, slots, tiles, field, ghost, table, put):
    @pl.loop(first, last)
    def _(r):
        degree = degrees[r]
        share = lax.rsqrt(jnp.full((1, WIDTH), degree.astype(F32)))
        total = jnp.zeros((BS, WIDTH), F32)
        for t in range(DEPTH // GROUP):
            entries = range(t * GROUP, (t + 1) * GROUP)
            left = jnp.concatenate(
                [table[jnp.where(k < degree, tiles[r, k], 16)] for k in entries], axis=1
            )
            right = jnp.concatenate([ghost[slots[r, k]] for k in entries], axis=0)
            total = total + jnp.dot(left, right, preferred_element_type=F32)
        put(r, (field[r].astype(F32) + share * total).astype(BF16))


def widen_scratch():
    return [DMA((PARTS, 3)), DMA((PARTS, 3)), DMA((PARTS, 4)), DMA((PARTS, 4))]


class Widen:
    def __init__(self, place, wide, scratch):
        self.f = place[2]
        self.node = lax.axis_index("nodes")
        self.wide = wide
        self.sems = scratch
        self.far, self.near = {}, {}

    def piece(self, owner, q):
        return self.wide.at[owner, pl.ds(q * PART, PART)]

    def push(self, q):
        xs, xr = self.sems[:2]
        mine = self.piece(self.f, q)
        for i, dx in enumerate((1, 3, 2)):
            copy = send(
                mine, mine, xs.at[q, i], xr.at[q, i], (self.node, feat_at(self.f, dx, 0))
            )
            copy.start()
            self.far[q, i] = copy
        self.pass_on(q, 3, self.f)

    def pass_on(self, q, i, owner):
        cs, cr = self.sems[2:]
        block = self.piece(owner, q)
        copy = send(
            block, block, cs.at[q, i], cr.at[q, i], (self.node, feat_at(self.f, 0, 1))
        )
        copy.start()
        self.near[q, i] = copy

    def relay(self, q):
        for i, dx in enumerate((3, 1, 2)):
            self.far[q, i].wait_recv()
            self.pass_on(q, i, feat_at(self.f, dx, 0))

    def ready(self, q):
        for i in range(4):
            self.near[q, i].wait_recv()

    def finish(self):
        for copy in list(self.far.values()) + list(self.near.values()):
            copy.wait_send()


TO_ABOVE = [(4, 0), (3, 0), (3, 1), (2, 0), (2, 1), (1, 0), (1, 1)]
TO_BELOW = [(4, 1), (5, 1), (5, 0), (6, 1), (6, 0), (7, 1), (7, 0)]


def settle_scratch():
    return [
        pltpu.VMEM((RING, 3, 2, BS, WIDTH), BF16),
        pltpu.VMEM((RING, BLKS, BS, WIDTH), BF16),
        pltpu.VMEM((2, 7, 4, BS, WIDTH), BF16),
        DMA((RING, 3)),
        DMA((RING, 3)),
        DMA((2, 7)),
        DMA((2, 7)),
    ]


def settle_stages(place, partial, table, own, wide, scratch):
    y, z, f = place
    landed, held, came, ys, yr, zs, zr = scratch
    above, below = (node_at(y, z, 0, 1), f), (node_at(y, z, 0, -1), f)
    across = {}
    for o in (4, 3, 5, 2, 6, 1, 7, 0):
        zz = lax.rem(z + o, RING)
        for dy in (1, 3, 2):
            owner = lax.rem(y + dy, ROWS)
            copy = send(
                partial.at[pl.ds((owner * RING + zz) * 2, 2)],
                landed.at[o, dy - 1],
                ys.at[o, dy - 1],
                yr.at[o, dy - 1],
                (node_at(y, z, dy, 0), f),
            )
            copy.start()
            across[o, dy] = copy
    yield

    def gathered(o, h, extras):
        zz = lax.rem(z + o, RING)
        sources, where = [], []
        for dy in range(ROWS):
            reader = lax.rem(y + ROWS - dy, ROWS)
            for j in range(2):
                where.append(wanted(table, y, reader, j, zz))
                sources.append((dy, j))
        marks = [
            [jnp.where(where[i] == 4 * h + b, 1.0, 0.0).astype(F32) for i in range(8)]
            for b in range(4)
        ]
        first = (y * RING + zz) * 2

        @pl.loop(0, BS // 16)
        def _(t):
            rows = pl.ds(pl.multiple_of(t * 16, 16), 16)
            values = []
            for dy, j in sources:
                if dy == 0:
                    value = partial[first + j, rows, :]
                else:
                    value = landed[o, dy - 1, j, rows, :]
                values.append(value.astype(F32))
            for b in range(4):
                block = 4 * h + b
                total = marks[b][0] * values[0]
                for i in range(1, 8):
                    total = total + marks[b][i] * values[i]
                for lane, index in extras:
                    total = total + came[lane, index, b, rows, :].astype(F32)
                if o == 0:
                    total = total + own[block, rows, :].astype(F32)
                    flat = pl.ds(pl.multiple_of(block * BS + t * 16, 16), 16)
                    wide[f, flat, :] = total.astype(BF16)
                else:
                    held[o, block, rows, :] = total.astype(BF16)

    def piece(lane, index, o, h):
        return send(
            held.at[o, pl.ds(4 * h, 4)],
            came.at[lane, index],
            zs.at[lane, index],
            zr.at[lane, index],
            above if lane == 0 else below,
        )

    def feeds(lane, o, h):
        lists = (TO_ABOVE, TO_BELOW)
        source = (o + (1 if lane == 0 else -1)) % 8
        return [(lane, i) for i, item in enumerate(lists[lane]) if item == (source, h)]

    pieces = {}

    def land(o):
        for dy in (1, 2, 3):
            across[o, dy].wait_recv()

    def forward(lane, index):
        o, h = (TO_ABOVE, TO_BELOW)[lane][index]
        extras = feeds(lane, o, h)
        for key in extras:
            pieces[key].wait_recv()
        gathered(o, h, extras)
        pieces[lane, index] = piece(lane, index, o, h)
        pieces[lane, index].start()

    land(4)
    forward(0, 0)
    forward(1, 0)
    yield
    for turn, (a, b) in enumerate(((3, 5), (2, 6), (1, 7))):
        land(a)
        land(b)
        for half in range(2):
            forward(0, 1 + 2 * turn + half)
            forward(1, 1 + 2 * turn + half)
            yield
    land(0)
    for half in range(2):
        extras = feeds(0, 0, half) + feeds(1, 0, half)
        for key in extras:
            pieces[key].wait_recv()
        gathered(0, half, extras)
        yield
    for copy in list(across.values()) + list(pieces.values()):
        copy.wait_send()
    yield


def times(wide, weight, rows):
    total = None
    for pair in range(FEAT // 2):
        left = jnp.concatenate([wide[2 * pair, rows, :], wide[2 * pair + 1, rows, :]], axis=1)
        right = jnp.concatenate([weight[2 * pair], weight[2 * pair + 1]], axis=0)
        term = jnp.dot(left, right, preferred_element_type=F32)
        total = term if total is None else total + term
    return total


def times_turned(wide, weight, rows):
    total = None
    for pair in range(FEAT // 2):
        left = jnp.concatenate([wide[2 * pair, rows, :], wide[2 * pair + 1, rows, :]], axis=1)
        right = jnp.concatenate([weight[2 * pair], weight[2 * pair + 1]], axis=1)
        term = lax.dot_general(left, right, (((1,), (1,)), ((), ())), preferred_element_type=F32)
        total = term if total is None else total + term
    return total


def reduce_scratch():
    return [
        pltpu.VMEM((ROWS, 256, WIDTH), BF16),
        pltpu.VMEM((3, 256, WIDTH), BF16),
        pltpu.VMEM((RING, 32, WIDTH), F32),
        pltpu.VMEM((7, 32, WIDTH), F32),
        DMA((3,)),
        DMA((3,)),
        DMA((7,)),
        DMA((7,)),
    ]


def reduce_stages(place, wide, right, out, scratch):
    y, z, f = place
    shares, came, mine, landed, ys, yr, zs, zr = scratch
    across = []

    def fill(owner):
        for j in range(2):
            value = lax.dot_general(
                wide[2 * owner + j],
                right(),
                (((0,), (0,)), ((), ())),
                preferred_element_type=F32,
            )
            shares[owner, pl.ds(j * 128, 128), :] = value.astype(BF16)

    for dy in (2, 1, 3):
        owner = lax.rem(y + dy, ROWS)
        fill(owner)
        copy = send(
            shares.at[owner],
            came.at[dy - 1],
            ys.at[dy - 1],
            yr.at[dy - 1],
            (node_at(y, z, dy, 0), f),
        )
        copy.start()
        across.append(copy)
    fill(y)
    yield
    for copy in across:
        copy.wait_recv()
    for o in range(RING):
        rows = pl.ds(o * 32, 32)
        total = shares[y, rows, :].astype(F32)
        for i in range(3):
            total = total + came[i, rows, :].astype(F32)
        mine[o] = total
    along = []
    for dz in (4, 3, 5, 2, 6, 1, 7):
        copy = send(
            mine.at[lax.rem(z + dz, RING)],
            landed.at[dz - 1],
            zs.at[dz - 1],
            zr.at[dz - 1],
            (node_at(y, z, 0, dz), f),
        )
        copy.start()
        along.append(copy)
    yield
    for copy in along:
        copy.wait_recv()
    total = mine[z]
    for i in range(7):
        total = total + landed[i]
    out[...] = total
    for copy in across + along:
        copy.wait_send()
    yield


SIZES = (13, 13, 4, 4, 4, 7, 8, 8)


def whole_scratch():
    return (
        gather_scratch()
        + gather_scratch()
        + widen_scratch()
        + widen_scratch()
        + widen_scratch()
        + settle_scratch()
        + reduce_scratch()
        + reduce_scratch()
    )


def whole_kernel(
    degrees,
    slots,
    tile_ids,
    wants,
    field,
    cot,
    partial,
    tile_table,
    weight_one,
    weight_two,
    out,
    grad_one,
    grad_two,
    requests,
    table,
    tiles,
    two_rows,
    agg_wide,
    hidden_wide,
    back_wide,
    pre_one,
    mixed,
    back_pre,
    ts,
    tr,
    ws,
    wr,
    local,
    *scratch,
):
    place = y, z, f = whereabouts()
    node = lax.axis_index("nodes")
    cuts = [sum(SIZES[:i]) for i in range(len(SIZES) + 1)]
    groups = [scratch[cuts[i] : cuts[i + 1]] for i in range(len(SIZES))]
    column = [(node_at(y, z, dy, 0), f) for dy in (1, 2, 3)]
    along = [(node_at(y, z, 0, dz), f) for dz in range(1, RING)]
    feats = [(node, lax.rem(f + d, FEAT)) for d in range(1, FEAT)]
    greet(column + along + feats)

    asks = []
    for dy in (1, 2, 3):
        copy = send(wants, requests.at[y], ts.at[dy - 1], tr.at[dy - 1], column[dy - 1])
        copy.start()
        asks.append(copy)
    gather = gather_stages(place, field, table, groups[0])
    step(gather, gather)
    parts = []
    for d in range(1, FEAT):
        copy = send(
            weight_two.at[lax.rem(f + d, FEAT)],
            two_rows.at[f],
            ws.at[d - 1],
            wr.at[d - 1],
            feats[d - 1],
        )
        copy.start()
        parts.append(copy)
    two_rows[f] = weight_two[f]
    requests[y] = wants[...]
    for t in range(16):
        tiles[t] = tile_table[t]
    tiles[16] = jnp.zeros((BS, BS), BF16)
    for copy in asks:
        copy.wait_recv()
    move = pltpu.make_async_copy(requests, table, local)
    move.start()
    move.wait()
    for _ in range(8):
        step(gather)
    settle = settle_stages(place, partial, table, cot, back_wide, groups[5])
    step(settle)
    drain(gather)

    agg = Widen(place, agg_wide, groups[2])
    hid = Widen(place, hidden_wide, groups[3])
    for q in range(PARTS):

        def put(r, value):
            agg_wide[f, pl.ds(pl.multiple_of(r * BS, BS), BS), :] = value

        spread_rows(
            2 * q, 2 * q + 2, degrees, slots, tile_ids, field, groups[0][8], tiles, put
        )
        agg.push(q)

    def project(q):
        agg.ready(q)
        rows = pl.ds(q * PART, PART)
        pre = times(agg_wide, weight_one, rows)
        pre_one[rows, :] = pre
        hidden_wide[f, rows, :] = (pre * jax.nn.sigmoid(pre)).astype(BF16)
        hid.push(q)

    def mix(q):
        hid.ready(q)
        value = times(hidden_wide, weight_two, pl.ds(q * PART, PART)).astype(BF16)
        mixed[2 * q] = value[:BS]
        mixed[2 * q + 1] = value[BS:]

    agg.relay(0)
    step(settle)
    agg.relay(1)
    project(0)
    step(settle)
    agg.relay(2)
    project(1)
    step(settle)
    agg.relay(3)
    project(2)
    step(settle)
    project(3)
    hid.relay(0)
    step(settle)
    hid.relay(1)
    mix(0)
    step(settle)
    hid.relay(2)
    mix(1)
    second = gather_stages(place, mixed, table, groups[1])
    step(second)
    step(settle)
    hid.relay(3)
    mix(2)
    mix(3)
    step(second)

    back = Widen(place, back_wide, groups[4])
    step(settle)
    back.push(0)
    back.push(1)
    step(second)
    step(settle)
    back.push(2)
    back.push(3)
    step(second)

    two = reduce_stages(place, hidden_wide, lambda: back_wide[f], grad_two, groups[7])
    step(two)
    step(second)

    def backward(q):
        back.ready(q)
        rows = pl.ds(q * PART, PART)
        total = times_turned(back_wide, two_rows, rows)
        pre = pre_one[rows, :]
        sigma = jax.nn.sigmoid(pre)
        back_pre[rows, :] = (total * sigma * (1.0 + pre * (1.0 - sigma))).astype(BF16)

    for copy in parts:
        copy.wait()
    back.relay(0)
    back.relay(1)
    backward(0)
    step(second)
    back.relay(2)
    backward(1)
    step(second)
    back.relay(3)
    backward(2)
    backward(3)
    one = reduce_stages(place, agg_wide, lambda: back_pre[...], grad_one, groups[6])
    step(second)
    step(one)
    step(second)
    step(two)
    step(second)
    step(one)
    drain(second)

    def put_out(r, value):
        out[r] = value

    spread_rows(0, BLKS, degrees, slots, tile_ids, mixed, groups[1][8], tiles, put_out)
    drain(two)
    drain(one)
    drain(settle)
    for copy in asks:
        copy.wait_send()
    agg.finish()
    hid.finish()
    back.finish()


def whole(*operands):
    wide = pltpu.VMEM((FEAT, 1024, WIDTH), BF16)
    return pl.pallas_call(
        whole_kernel,
        out_shape=(
            jax.ShapeDtypeStruct((BLKS, BS, WIDTH), BF16),
            jax.ShapeDtypeStruct((32, WIDTH), F32),
            jax.ShapeDtypeStruct((32, WIDTH), F32),
        ),
        in_specs=[SMEM] * 3 + [VMEM] * 7,
        out_specs=(VMEM,) * 3,
        scratch_shapes=[
            pltpu.VMEM((ROWS, 2, 32), jnp.int32),
            pltpu.SMEM((ROWS, 2, 32), jnp.int32),
            pltpu.VMEM((17, BS, BS), BF16),
            pltpu.VMEM((FEAT, 128, WIDTH), BF16),
            wide,
            wide,
            wide,
            pltpu.VMEM((1024, WIDTH), F32),
            pltpu.VMEM((BLKS, BS, WIDTH), BF16),
            pltpu.VMEM((1024, WIDTH), BF16),
            DMA((3,)),
            DMA((3,)),
            DMA((7,)),
            DMA((7,)),
            DMA(()),
        ]
        + whole_scratch(),
        compiler_params=pltpu.CompilerParams(collective_id=0, has_side_effects=True),
    )(*operands)


def on_device(
    features, ghosts, slots, tile_ids, degrees, tile_table, weight_one, weight_two, cotangent
):
    blocks = features.reshape(BLKS, BS, WIDTH)
    cot = cotangent.reshape(BLKS, BS, WIDTH)
    one = weight_one.reshape(FEAT, 128, WIDTH)
    two = weight_two.reshape(FEAT, 128, WIDTH)
    partial = share_out(degrees, slots, tile_ids, cot, tile_table)
    output, grad_one, grad_two = whole(
        degrees, slots, tile_ids, ghosts.T, blocks, cot, partial, tile_table, one, two
    )
    return (output.reshape(1024, WIDTH), grad_one, grad_two)


def solution(mesh):
    return jax.shard_map(
        on_device,
        mesh=mesh,
        in_specs=(
            P("nodes", "feat"),
            P("nodes", None),
            P("nodes", None),
            P("nodes", None),
            P("nodes"),
            P(),
            P(None, "feat"),
            P(None, "feat"),
            P("nodes", "feat"),
        ),
        out_specs=(P("nodes", "feat"), P("nodes", "feat"), P("nodes", "feat")),
        check_vma=False,
    )
```

time: 173 us -> 126 us (0.73)
  Pallas kernels: 162 us -> 121 us
  other arithmetic: 3.72 us -> 0 us
    pallas_call x5 -> x2, Pallas kernels: 162 us -> 121 us  [the longest x1 113 us: whole(): pl.pallas_call(whole_kernel, out_shape=(jax.ShapeDtypeStruct((BLKS, BS, W...]
    unnamed x6 -> x3, local copies, waits for them, and re-layouts: 1.22 us -> 4.32 us
    select_n x2 -> x0, other arithmetic: 2.55 us -> none  [the longest x1 1.35 us: on_device(): live_tiles = jnp.where(position < degrees[:, None], tile_ids, 16)]
    pad x2 -> x0, local copies, waits for them, and re-layouts: 2.53 us -> none  [the longest x1 1.92 us: on_device(): table = jnp.pad(tile_table, ((0, 1), (0, 0), (0, 0)))]
where the time goes in v3:
time: 126 us
  Pallas kernels  121 us (96%)
  local copies, waits for them, and re-layouts  4.32 us (3%)
    pallas_call x1, Pallas kernels, whole(): pl.pallas_call(whole_kernel, out_shape=(jax.ShapeDtypeStruct((BLKS, BS, W...  113 us
    pallas_call x1, Pallas kernels, share_out(): pl.pallas_call(share_kernel, out_shape=jax.ShapeDtypeStruct((64, BS, WIDT...  7.5 us
    unnamed x3, local copies, waits for them, and re-layouts  4.32 us

profile of v3, /device:TPU:1, one launch (start us, length us, event | category | flops | bytes accessed | tf_op | source)
XLA Modules:
  0.0 125.6 jit_solution(8109270703454925724)
XLA Ops:
  0.6 7.5 %shard_map.112.partial = bf16[64,128,128]{2,1,0:T(8,128)(2,1)} custom-call(s32[8]{0:T(128)} %degrees.3, s32[8,24]{1,0:T(8,128)} %slots.3, s32[8,24]{1,0:T(8,128)} %tile_ids.1, bf16[8,128,128]{2,1,0:T(8,128)(2,1)} %bitcast.6, bf16[16,128,128]{2,1,0:T(8,128)(2,1)} %tile_table.1), custom_call_target="tpu_custom_call" | custom-call | tf_op jit(solution)/shard_map/pallas_call | solution.py:192
  8.1 113.2 %shard_map.113 = (bf16[8,128,128]{2,1,0:T(8,128)(2,1)}, f32[32,128]{1,0:T(8,128)}, f32[32,128]{1,0:T(8,128)}) custom-call(s32[8]{0:T(128)} %degrees.3, s32[8,24]{1,0:T(8,128)} %slots.3, s32[8,24]{1,0:T(8,128)} %tile_ids.1, s32[2,32]{1,0:T(2,128)} %bitcast.12, bf16[8,128,128]{2,1,0:T(8,128)(2,1)} %bitcast.8, bf16[8,128,128]{2,1,0:T(8,128)(2,1)} %bitcast.7, ...), custom_call_target="tpu_custom_call" | custom-call | tf_op jit(solution)/shard_map/pallas_call | solution.py:690
  121.3 1.7 %copy.15 = bf16[1024,128]{1,0:T(8,128)(2,1)} copy(bf16[1024,128]{1,0:T(8,128)(2,1)} %bitcast.11) | data formatting | bytes 524288
  123.0 1.3 %copy.16 = f32[32,128]{1,0:T(8,128)} copy(f32[32,128]{1,0:T(8,128)} %get-tuple-element.13) | data formatting | bytes 32768
  124.3 1.3 %copy.17 = f32[32,128]{1,0:T(8,128)} copy(f32[32,128]{1,0:T(8,128)} %get-tuple-element.14) | data formatting | bytes 32768
